TPU v7x, 512 devices: a whole 4x8x8 slice. The times are simulated.
512 devices in a mesh: gx: 32 (over x, z_hi, core), gy: 16 (over z_lo, y).
Axes of the slice: x: 4, y: 8, z: 8 (z_hi: 4, z_lo: 2; z = z_hi * 2 + z_lo), core: 2. Of those that a mesh axis runs over, the one named last changes fastest.
Arguments:
- coefficients: float32 [32, 16, 256, 1024], P('gx', 'gy'), may hold values from -6 to 6
- transfer_blocks: float32 [4, 32, 16, 256, 512], P(None, 'gx', 'gy'), may hold values from -0.25 to 0.25
Outputs:
- result_blocks: float32 [32, 16, 256, 1024], P('gx', 'gy')
All inputs are finite; a program needn't handle non-finite values.
Results may differ from a plain program's by a relative error of at most 0.0001.
Values sent between devices are 32-bit elements; how exact they have to be, the bound alone decides.
No kernel may reach another device: no remote copies, remote signals or barrier semaphores. Data moves between devices by JAX's collectives and lax.ppermute only.
A program may use at most 64 MiB of HBM per device.

v0:
```python
import jax
import jax.numpy as jnp
from jax import lax
from jax.sharding import PartitionSpec as P


def partner_2(block, axis, bit):
    count = lax.axis_size(axis)
    route = []
    for low in range(count):
        high = low | 1 << bit
        if high != low and high < count:
            route += [(low, high), (high, low)]
    return lax.ppermute(block, axis, route)


def matmul(left, right):
    return jnp.dot(left, right, preferred_element_type=jnp.float32, precision=lax.Precision.HIGHEST)


def swap_high(state, bit_number):
    return partner_2(state, "gx", bit_number)


def swap_low(state, bit_number):
    return partner_2(state, "gy", bit_number)


def one_level(state, block, swapper, bit_number, upper_bit):
    partner = swapper(state, bit_number)
    lower_block = jnp.where(upper_bit == 0, state, partner)
    upper_block = jnp.where(upper_bit == 0, partner, state)
    stacked = jnp.concatenate([lower_block, upper_block], axis=0)
    return matmul(block, stacked)


def on_device(coefficients, transfer_blocks):
    state = coefficients[0, 0]
    blocks = transfer_blocks[:, 0, 0]
    high_top = lax.axis_size("gx").bit_length() - 2
    low_top = lax.axis_size("gy").bit_length() - 2
    high_index = lax.axis_index("gx")
    low_index = lax.axis_index("gy")
    plan = [("high", high_top), ("low", low_top), ("high", high_top - 1), ("low", low_top - 1)]
    for level_number in range(4):
        which, bit_number = plan[level_number]
        if which == "high":
            upper_bit = jnp.bitwise_and(jnp.right_shift(high_index, bit_number), 1)
            swapper = swap_high
        else:
            upper_bit = jnp.bitwise_and(jnp.right_shift(low_index, bit_number), 1)
            swapper = swap_low
        state = one_level(state, blocks[level_number], swapper, bit_number, upper_bit)
    return state[None, None]


def solution(mesh):
    in_specs = (P("gx", "gy", None, None), P(None, "gx", "gy", None, None))
    out_specs = P("gx", "gy", None, None)
    return jax.shard_map(
        on_device, mesh=mesh, in_specs=in_specs, out_specs=out_specs, check_vma=False
    )
```

profile of v0, /device:TPU:166, one launch (start us, length us, event | category | flops | bytes accessed | tf_op | source)
XLA Modules:
  0.0 148.4 jit_solution(11372157622136940193)
XLA Ops:
  0.0 3.3 %collective-permute-start = (f32[256,1024]{1,0:T(8,128)}, f32[256,1024]{1,0:T(8,128)S(1)}, u32[]{:S(2)}, u32[]{:S(2)}) collective-permute-start(f32[256,1024]{1,0:T(8,128)} %bitcast.25), channel_id=1, source_target_pairs={{0,256},{256,0},{16,272},{272,16},{32,288},{288,32},{48,304},{304,... | collective-permute-start | bytes 3145736 | tf_op jit(solution)/shard_map/ppermute | solution.py:14
  3.3 0.0 copy-start
  3.3 25.2 %collective-permute-done = f32[256,1024]{1,0:T(8,128)S(1)} collective-permute-done((f32[256,1024]{1,0:T(8,128)}, f32[256,1024]{1,0:T(8,128)S(1)}, u32[]{:S(2)}, u32[]{:S(2)}) %collective-permute-start) | collective-permute-done | bytes 1048608 | tf_op jit(solution)/shard_map/ppermute | solution.py:14
  28.5 1.4 broadcast_select_fusion.1
  29.9 0.0 copy-done
  29.9 2.0 %fusion.25 = f32[256,1024]{1,0:T(8,128)S(1)} fusion(f32[256,1024]{1,0:T(8,128)S(1)} %get-tuple-element.12, f32[256,1024]{1,0:T(8,128)S(1)} %get-tuple-element.11, f32[4,1,1,256,512]{4,3,2,1,0:T(8,128)S(1)} %copy-done), kind=kOutput, calls=%fused_computation.19 | convolution fusion | flops 1611137024 | bytes 3670016 | tf_op jit(solution)/shard_map/dot_general | solution.py:18
  31.9 4.3 %collective-permute-start.1 = (f32[256,1024]{1,0:T(8,128)S(1)}, f32[256,1024]{1,0:T(8,128)}, u32[]{:S(2)}, u32[]{:S(2)}) collective-permute-start(f32[256,1024]{1,0:T(8,128)S(1)} %fusion.25), channel_id=1, source_target_pairs={{0,8},{8,0},{1,9},{9,1},{2,10},{10,2},{3,11},{11,3},{4,12},{12,4},... | collective-permute-start | bytes 3145736 | tf_op jit(solution)/shard_map/ppermute | solution.py:14
  36.2 22.4 %collective-permute-done.1 = f32[256,1024]{1,0:T(8,128)} collective-permute-done((f32[256,1024]{1,0:T(8,128)S(1)}, f32[256,1024]{1,0:T(8,128)}, u32[]{:S(2)}, u32[]{:S(2)}) %collective-permute-start.1) | collective-permute-done | bytes 1048608 | tf_op jit(solution)/shard_map/ppermute | solution.py:14
  58.6 1.4 broadcast_select_fusion.3
  60.0 2.0 %fusion.22 = f32[256,1024]{1,0:T(8,128)S(1)} fusion(f32[256,1024]{1,0:T(8,128)S(1)} %get-tuple-element.10, f32[256,1024]{1,0:T(8,128)S(1)} %get-tuple-element.9, f32[4,1,1,256,512]{4,3,2,1,0:T(8,128)S(1)} %copy-done), kind=kOutput, calls=%fused_computation.18 | convolution fusion | flops 1611137024 | bytes 3670016 | tf_op jit(solution)/shard_map/dot_general | solution.py:18
  62.0 2.7 %collective-permute-start.2 = (f32[256,1024]{1,0:T(8,128)S(1)}, f32[256,1024]{1,0:T(8,128)}, u32[]{:S(2)}, u32[]{:S(2)}) collective-permute-start(f32[256,1024]{1,0:T(8,128)S(1)} %fusion.22), channel_id=1, source_target_pairs={{0,128},{128,0},{16,144},{144,16},{32,160},{160,32},{48,176},{176,... | collective-permute-start | bytes 3145736 | tf_op jit(solution)/shard_map/ppermute | solution.py:14
  64.8 22.7 %collective-permute-done.2 = f32[256,1024]{1,0:T(8,128)} collective-permute-done((f32[256,1024]{1,0:T(8,128)S(1)}, f32[256,1024]{1,0:T(8,128)}, u32[]{:S(2)}, u32[]{:S(2)}) %collective-permute-start.2) | collective-permute-done | bytes 1048608 | tf_op jit(solution)/shard_map/ppermute | solution.py:14
  87.5 1.4 broadcast_select_fusion.5
  88.9 2.0 %fusion.19 = f32[256,1024]{1,0:T(8,128)S(1)} fusion(f32[256,1024]{1,0:T(8,128)S(1)} %get-tuple-element.8, f32[256,1024]{1,0:T(8,128)S(1)} %get-tuple-element.7, f32[4,1,1,256,512]{4,3,2,1,0:T(8,128)S(1)} %copy-done), kind=kOutput, calls=%fused_computation.17 | convolution fusion | flops 1611137024 | bytes 3670016 | tf_op jit(solution)/shard_map/dot_general | solution.py:18
  90.9 2.0 %collective-permute-start.3 = (f32[256,1024]{1,0:T(8,128)S(1)}, f32[256,1024]{1,0:T(8,128)}, u32[]{:S(2)}, u32[]{:S(2)}) collective-permute-start(f32[256,1024]{1,0:T(8,128)S(1)} %fusion.19), channel_id=1, source_target_pairs={{0,4},{4,0},{1,5},{5,1},{2,6},{6,2},{3,7},{7,3},{8,12},{12,8},{9,1... | collective-permute-start | bytes 3145736 | tf_op jit(solution)/shard_map/ppermute | solution.py:14
  93.0 49.2 %collective-permute-done.3 = f32[256,1024]{1,0:T(8,128)} collective-permute-done((f32[256,1024]{1,0:T(8,128)S(1)}, f32[256,1024]{1,0:T(8,128)}, u32[]{:S(2)}, u32[]{:S(2)}) %collective-permute-start.3) | collective-permute-done | bytes 1048608 | tf_op jit(solution)/shard_map/ppermute | solution.py:14
  142.2 1.4 broadcast_select_fusion.7
  143.6 3.5 %fusion.16 = f32[1,1,256,1024]{2,3,1,0:T(8,128)S(1)} fusion(f32[256,1024]{1,0:T(8,128)S(1)} %get-tuple-element.6, f32[256,1024]{1,0:T(8,128)S(1)} %get-tuple-element.5, f32[4,1,1,256,512]{4,3,2,1,0:T(8,128)S(1)} %copy-done), kind=kOutput, calls=%fused_computation.16 | convolution fusion | flops 1611137024 | bytes 3670016 | tf_op jit(solution)/shard_map/dot_general | solution.py:18
  147.1 1.3 copy.3
Async XLA Ops:
  0.0 28.5 %collective-permute-start = (f32[256,1024]{1,0:T(8,128)}, f32[256,1024]{1,0:T(8,128)S(1)}, u32[]{:S(2)}, u32[]{:S(2)}) collective-permute-start(f32[256,1024]{1,0:T(8,128)} %bitcast.25), channel_id=1, source_target_pairs={{0,256},{256,0},{16,272},{272,16},{32,288},{288,32},{48,304},{304,... | collective-permute-start | bytes 3145736 | tf_op jit(solution)/shard_map/ppermute | solution.py:14
  3.3 26.6 %copy-start = (f32[4,1,1,256,512]{4,3,2,1,0:T(8,128)S(1)}, f32[4,1,1,256,512]{4,3,2,1,0:T(8,128)}, u32[]{:S(2)}) copy-start(f32[4,1,1,256,512]{4,3,2,1,0:T(8,128)} %param.3) | copy-start | bytes 6291460
  31.9 26.7 %collective-permute-start.1 = (f32[256,1024]{1,0:T(8,128)S(1)}, f32[256,1024]{1,0:T(8,128)}, u32[]{:S(2)}, u32[]{:S(2)}) collective-permute-start(f32[256,1024]{1,0:T(8,128)S(1)} %fusion.25), channel_id=1, source_target_pairs={{0,8},{8,0},{1,9},{9,1},{2,10},{10,2},{3,11},{11,3},{4,12},{12,4},... | collective-permute-start | bytes 3145736 | tf_op jit(solution)/shard_map/ppermute | solution.py:14
  62.0 25.5 %collective-permute-start.2 = (f32[256,1024]{1,0:T(8,128)S(1)}, f32[256,1024]{1,0:T(8,128)}, u32[]{:S(2)}, u32[]{:S(2)}) collective-permute-start(f32[256,1024]{1,0:T(8,128)S(1)} %fusion.22), channel_id=1, source_target_pairs={{0,128},{128,0},{16,144},{144,16},{32,160},{160,32},{48,176},{176,... | collective-permute-start | bytes 3145736 | tf_op jit(solution)/shard_map/ppermute | solution.py:14
  90.9 51.2 %collective-permute-start.3 = (f32[256,1024]{1,0:T(8,128)S(1)}, f32[256,1024]{1,0:T(8,128)}, u32[]{:S(2)}, u32[]{:S(2)}) collective-permute-start(f32[256,1024]{1,0:T(8,128)S(1)} %fusion.19), channel_id=1, source_target_pairs={{0,4},{4,0},{1,5},{5,1},{2,6},{6,2},{3,7},{7,3},{8,12},{12,8},{9,1... | collective-permute-start | bytes 3145736 | tf_op jit(solution)/shard_map/ppermute | solution.py:14
where the time goes:
time: 149 us; the launch traced here: 148 us
  waiting for transfers between devices  119 us (80%)
  starting transfers between devices  12.3 us (8%)
  matrix products  9.55 us (6%)
  other arithmetic  5.63 us (4%)
    ppermute x4, waiting for transfers between devices, partner_2(): return lax.ppermute(block, axis, route)  119 us
    ppermute x4, starting transfers between devices, partner_2(): return lax.ppermute(block, axis, route)  12.3 us
    dot_general x4, matrix products, matmul(): jnp.dot(left, right, preferred_element_type=jnp.float32, precision=lax.Pr...  9.55 us
    select_n x4, other arithmetic, one_level(): lower_block = jnp.where(upper_bit == 0, state, partner)  5.63 us
  transfers between devices with their start and end apart: 4, of which 4 were waited for; matrix products, arithmetic and copies ran while one was open for 0% of the time, Pallas kernels for 0%

commit v1 on v0

v1 whole, which is shorter than its diff:
```python
import jax
import jax.numpy as jnp
from jax import lax
from jax.sharding import PartitionSpec as P


WIDTHS = (2, 3, 3)
ORDER = ((0, 0), (0, 1), (0, 2), (1, 0), (1, 1), (2, 0), (1, 2), (2, 1), (3, 0), (3, 1), (2, 2), (3, 2))


def plan():
    high_top = lax.axis_size("gx").bit_length() - 2
    low_top = lax.axis_size("gy").bit_length() - 2
    return [("gx", high_top), ("gy", low_top), ("gx", high_top - 1), ("gy", low_top - 1)]


def exchange(block, axis, bit):
    route = [(i, i ^ (1 << bit)) for i in range(lax.axis_size(axis))]
    return lax.ppermute(block, axis, route)


def dot(left, right):
    return jnp.dot(left, right, preferred_element_type=jnp.float32, precision=lax.Precision.HIGH)


def on_device(coefficients, transfer_blocks):
    state = coefficients[0, 0]
    rank, columns = state.shape
    edges = [0]
    for width in WIDTHS:
        edges.append(edges[-1] + width * (columns // 8))
    levels = plan()
    halves = []
    for level, (axis, bit) in enumerate(levels):
        block = transfer_blocks[level, 0, 0]
        upper = jnp.bitwise_and(jnp.right_shift(lax.axis_index(axis), bit), 1)
        mine = lax.dynamic_slice(block, (0, upper * rank), (rank, rank))
        other = lax.dynamic_slice(block, (0, (1 - upper) * rank), (rank, rank))
        halves.append((mine, other))
    pieces = [state[:, a:b] for a, b in zip(edges, edges[1:])]
    for level, piece in ORDER:
        axis, bit = levels[level]
        mine, other = halves[level]
        here = pieces[piece]
        there = exchange(here, axis, bit)
        pieces[piece] = dot(mine, here) + dot(other, there)
    return jnp.concatenate(pieces, axis=1).reshape(coefficients.shape)


def solution(mesh):
    in_specs = (P("gx", "gy", None, None), P(None, "gx", "gy", None, None))
    out_specs = P("gx", "gy", None, None)
    return jax.shard_map(
        on_device, mesh=mesh, in_specs=in_specs, out_specs=out_specs, check_vma=False
    )
```

time: 149 us -> 114 us (0.77)
  the two profiles are of different devices: /device:TPU:166 before, /device:TPU:128 now
where the time goes in v1:
time: 114 us; the launch traced here: 113 us
  starting transfers between devices  49.2 us (43%)
  waiting for transfers between devices  42.7 us (37%)
  matrix products  14.3 us (13%)
  local copies, waits for them, and re-layouts  5.18 us (5%)
    ppermute x12, starting transfers between devices, exchange(): return lax.ppermute(block, axis, route)  49.2 us
    ppermute x12, waiting for transfers between devices, exchange(): return lax.ppermute(block, axis, route)  42.7 us
    dot_general x24, matrix products, dot(): jnp.dot(left, right, preferred_element_type=jnp.float32, precision=lax.Pr...  14.3 us
    slice x2, local copies, waits for them, and re-layouts, on_device(): pieces = [state[:, a:b] for a, b in zip(edges, edges[1:])]  3.85 us
  transfers between devices with their start and end apart: 12, of which 7 were waited for; matrix products, arithmetic and copies ran while one was open for 14% of the time, Pallas kernels for 0%

profile of v1, /device:TPU:128, one launch (start us, length us, event | category | flops | bytes accessed | tf_op | source)
XLA Modules:
  0.0 112.9 jit_solution(1323717941113841609)
XLA Ops:
  0.0 2.2 %fusion.88 = (f32[256,384]{1,0:T(8,128)}, f32[256,384]{1,0:T(8,128)}) fusion(f32[256,1024]{1,0:T(8,128)} %bitcast.80), kind=kLoop, calls=%fused_computation.101 | loop fusion | bytes 1572864 | tf_op jit(solution)/shard_map/slice | solution.py:40
  2.2 4.9 %collective-permute-start.8 = (f32[256,384]{1,0:T(8,128)}, f32[256,384]{1,0:T(8,128)}, u32[]{:S(2)}, u32[]{:S(2)}) collective-permute-start(f32[256,384]{1,0:T(8,128)} %get-tuple-element.10), channel_id=1, source_target_pairs={{0,256},{16,272},{32,288},{48,304},{64,320},{80,336},{96,352},{112... | collective-permute-start | bytes 1179656 | tf_op jit(solution)/shard_map/ppermute | solution.py:19
  7.1 2.4 %collective-permute-start.4 = (f32[256,384]{1,0:T(8,128)}, f32[256,384]{1,0:T(8,128)}, u32[]{:S(2)}, u32[]{:S(2)}) collective-permute-start(f32[256,384]{1,0:T(8,128)} %get-tuple-element.9), channel_id=1, source_target_pairs={{0,256},{16,272},{32,288},{48,304},{64,320},{80,336},{96,352},{112... | collective-permute-start | bytes 1179656 | tf_op jit(solution)/shard_map/ppermute | solution.py:19
  9.5 1.7 %slice.28 = f32[256,256]{1,0:T(8,128)} slice(f32[256,1024]{1,0:T(8,128)} %bitcast.81), slice={[0:256], [0:256]} | slice | bytes 524288 | tf_op jit(solution)/shard_map/slice | solution.py:40
  11.2 4.9 %collective-permute-start = (f32[256,256]{1,0:T(8,128)}, f32[256,256]{1,0:T(8,128)}, u32[]{:S(2)}, u32[]{:S(2)}) collective-permute-start(f32[256,256]{1,0:T(8,128)} %slice.28), channel_id=1, source_target_pairs={{0,256},{16,272},{32,288},{48,304},{64,320},{80,336},{96,352},{112... | collective-permute-start | bytes 786440 | tf_op jit(solution)/shard_map/ppermute | solution.py:19
  16.2 0.2 fusion.87
  16.3 1.0 copy-done
  17.4 0.4 fusion.12
  17.8 1.0 fusion.16
  18.7 0.4 fusion.14
  19.1 11.7 %collective-permute-done = f32[256,256]{1,0:T(8,128)} collective-permute-done((f32[256,256]{1,0:T(8,128)}, f32[256,256]{1,0:T(8,128)}, u32[]{:S(2)}, u32[]{:S(2)}) %collective-permute-start) | collective-permute-done | bytes 262176 | tf_op jit(solution)/shard_map/ppermute | solution.py:19
  30.8 1.3 %convolution_add_fusion.11 = f32[256,256]{1,0:T(8,128)S(1)} fusion(f32[256,256]{1,0:T(8,128)} %fusion.16, f32[256,256]{1,0:T(8,128)} %collective-permute-done, f32[1,1,1,256,512]{4,3,2,1,0:T(8,128)S(1)} %get-tuple-element.7, s32[]{:T(128)S(6)} %select_n.28), kind=kOutput, calls=%fused_computation.11 | convolution fusion | flops 100728832 | bytes 1048580 | tf_op jit(solution)/shard_map/dot_general | solution.py:23
  32.1 4.3 %collective-permute-start.1 = (f32[256,256]{1,0:T(8,128)S(1)}, f32[256,256]{1,0:T(8,128)S(1)}, u32[]{:S(2)}, u32[]{:S(2)}) collective-permute-start(f32[256,256]{1,0:T(8,128)S(1)} %convolution_add_fusion.11), channel_id=1, source_target_pairs={{0,8},{1,9},{2,10},{3,11},{4,12},{5,13},{6,14},{7,15},{8,0},{9,1},... | collective-permute-start | bytes 786440 | tf_op jit(solution)/shard_map/ppermute | solution.py:19
  36.4 0.3 fusion.22
  36.7 1.4 %convolution_add_fusion.3 = f32[256,384]{1,0:T(8,128)S(1)} fusion(f32[256,384]{1,0:T(8,128)S(1)} %fusion.12, f32[256,384]{1,0:T(8,128)} %collective-permute-done.8, f32[1,1,1,256,512]{4,3,2,1,0:T(8,128)S(1)} %get-tuple-element.7, s32[]{:T(128)S(6)} %select_n.28), kind=kOutput, calls=%fused_computation.3 | convolution fusion | flops 151093248 | bytes 1441796 | tf_op jit(solution)/shard_map/dot_general | solution.py:23
  38.1 0.4 fusion.18
  38.5 1.9 %collective-permute-start.9 = (f32[256,384]{1,0:T(8,128)S(1)}, f32[256,384]{1,0:T(8,128)S(1)}, u32[]{:S(2)}, u32[]{:S(2)}) collective-permute-start(f32[256,384]{1,0:T(8,128)S(1)} %convolution_add_fusion.3), channel_id=1, source_target_pairs={{0,8},{1,9},{2,10},{3,11},{4,12},{5,13},{6,14},{7,15},{8,0},{9,1},... | collective-permute-start | bytes 1179656 | tf_op jit(solution)/shard_map/ppermute | solution.py:19
  40.4 1.4 %convolution_add_fusion.7 = f32[256,384]{1,0:T(8,128)S(1)} fusion(f32[256,384]{1,0:T(8,128)S(1)} %fusion.14, f32[256,384]{1,0:T(8,128)} %collective-permute-done.4, f32[1,1,1,256,512]{4,3,2,1,0:T(8,128)S(1)} %get-tuple-element.7, s32[]{:T(128)S(6)} %select_n.28), kind=kOutput, calls=%fused_computation.7 | convolution fusion | flops 151093248 | bytes 1441796 | tf_op jit(solution)/shard_map/dot_general | solution.py:23
  41.8 0.9 collective-permute-done.1
  42.7 0.3 convolution_add_fusion.10
  43.0 3.4 %collective-permute-start.2 = (f32[256,256]{1,0:T(8,128)S(1)}, f32[256,256]{1,0:T(8,128)S(1)}, u32[]{:S(2)}, u32[]{:S(2)}) collective-permute-start(f32[256,256]{1,0:T(8,128)S(1)} %convolution_add_fusion.10), channel_id=1, source_target_pairs={{0,128},{16,144},{32,160},{48,176},{64,192},{80,208},{96,224},{112... | collective-permute-start | bytes 786440 | tf_op jit(solution)/shard_map/ppermute | solution.py:19
  46.4 0.4 fusion.20
  46.7 4.4 %collective-permute-start.5 = (f32[256,384]{1,0:T(8,128)S(1)}, f32[256,384]{1,0:T(8,128)S(1)}, u32[]{:S(2)}, u32[]{:S(2)}) collective-permute-start(f32[256,384]{1,0:T(8,128)S(1)} %convolution_add_fusion.7), channel_id=1, source_target_pairs={{0,8},{1,9},{2,10},{3,11},{4,12},{5,13},{6,14},{7,15},{8,0},{9,1},... | collective-permute-start | bytes 1179656 | tf_op jit(solution)/shard_map/ppermute | solution.py:19
  51.2 0.3 fusion.28
  51.4 0.3 convolution_add_fusion.9
  51.7 7.7 %collective-permute-start.3 = (f32[256,256]{1,0:T(8,128)S(1)}, f32[256,256]{1,0:T(8,128)S(1)}, u32[]{:S(2)}, u32[]{:S(2)}) collective-permute-start(f32[256,256]{1,0:T(8,128)S(1)} %convolution_add_fusion.9), channel_id=1, source_target_pairs={{0,4},{1,5},{2,6},{3,7},{4,0},{5,1},{6,2},{7,3},{8,12},{9,13},{10,... | collective-permute-start | bytes 786440 | tf_op jit(solution)/shard_map/ppermute | solution.py:19
  59.5 0.4 fusion.34
  59.9 0.4 convolution_add_fusion.2
  60.3 3.2 %collective-permute-start.10 = (f32[256,384]{1,0:T(8,128)S(1)}, f32[256,384]{1,0:T(8,128)}, u32[]{:S(2)}, u32[]{:S(2)}) collective-permute-start(f32[256,384]{1,0:T(8,128)S(1)} %convolution_add_fusion.2), channel_id=1, source_target_pairs={{0,128},{16,144},{32,160},{48,176},{64,192},{80,208},{96,224},{112... | collective-permute-start | bytes 1179656 | tf_op jit(solution)/shard_map/ppermute | solution.py:19
  63.5 0.4 fusion.24
  63.8 0.4 convolution_add_fusion.6
  64.2 2.7 %collective-permute-start.6 = (f32[256,384]{1,0:T(8,128)S(1)}, f32[256,384]{1,0:T(8,128)}, u32[]{:S(2)}, u32[]{:S(2)}) collective-permute-start(f32[256,384]{1,0:T(8,128)S(1)} %convolution_add_fusion.6), channel_id=1, source_target_pairs={{0,128},{16,144},{32,160},{48,176},{64,192},{80,208},{96,224},{112... | collective-permute-start | bytes 1179656 | tf_op jit(solution)/shard_map/ppermute | solution.py:19
  67.0 0.4 fusion.26
  67.3 0.3 collective-permute-done.3
  67.6 0.4 convolution_add_fusion.8
  68.1 5.9 %collective-permute-done.10 = f32[256,384]{1,0:T(8,128)} collective-permute-done((f32[256,384]{1,0:T(8,128)S(1)}, f32[256,384]{1,0:T(8,128)}, u32[]{:S(2)}, u32[]{:S(2)}) %collective-permute-start.10) | collective-permute-done | bytes 393248 | tf_op jit(solution)/shard_map/ppermute | solution.py:19
  74.0 1.4 %convolution_add_fusion.1 = f32[256,384]{1,0:T(8,128)S(1)} fusion(f32[256,384]{1,0:T(8,128)S(1)} %fusion.24, f32[256,384]{1,0:T(8,128)} %collective-permute-done.10, f32[1,1,1,256,512]{4,3,2,1,0:T(8,128)S(1)} %get-tuple-element.6, s32[]{:T(128)S(6)} %select_n.30), kind=kOutput, calls=%fused_computation.1 | convolution fusion | flops 151093248 | bytes 1441796 | tf_op jit(solution)/shard_map/dot_general | solution.py:23
  75.4 2.4 %collective-permute-start.11 = (f32[256,384]{1,0:T(8,128)S(1)}, f32[256,384]{1,0:T(8,128)S(1)}, u32[]{:S(2)}, u32[]{:S(2)}) collective-permute-start(f32[256,384]{1,0:T(8,128)S(1)} %convolution_add_fusion.1), channel_id=1, source_target_pairs={{0,4},{1,5},{2,6},{3,7},{4,0},{5,1},{6,2},{7,3},{8,12},{9,13},{10,... | collective-permute-start | bytes 1179656 | tf_op jit(solution)/shard_map/ppermute | solution.py:19
  77.8 0.4 collective-permute-done.6
  78.2 1.4 %convolution_add_fusion.5 = f32[256,384]{1,0:T(8,128)S(1)} fusion(f32[256,384]{1,0:T(8,128)S(1)} %fusion.26, f32[256,384]{1,0:T(8,128)} %collective-permute-done.6, f32[1,1,1,256,512]{4,3,2,1,0:T(8,128)S(1)} %get-tuple-element.6, s32[]{:T(128)S(6)} %select_n.30), kind=kOutput, calls=%fused_computation.5 | convolution fusion | flops 151093248 | bytes 1441796 | tf_op jit(solution)/shard_map/dot_general | solution.py:23
  79.6 7.0 %collective-permute-start.7 = (f32[256,384]{1,0:T(8,128)S(1)}, f32[256,384]{1,0:T(8,128)S(1)}, u32[]{:S(2)}, u32[]{:S(2)}) collective-permute-start(f32[256,384]{1,0:T(8,128)S(1)} %convolution_add_fusion.5), channel_id=1, source_target_pairs={{0,4},{1,5},{2,6},{3,7},{4,0},{5,1},{6,2},{7,3},{8,12},{9,13},{10,... | collective-permute-start | bytes 1179656 | tf_op jit(solution)/shard_map/ppermute | solution.py:19
  86.6 0.4 fusion.30
  87.0 0.4 fusion.32
  87.3 19.8 %collective-permute-done.11 = f32[256,384]{1,0:T(8,128)S(1)} collective-permute-done((f32[256,384]{1,0:T(8,128)S(1)}, f32[256,384]{1,0:T(8,128)S(1)}, u32[]{:S(2)}, u32[]{:S(2)}) %collective-permute-start.11) | collective-permute-done | bytes 393248 | tf_op jit(solution)/shard_map/ppermute | solution.py:19
  107.1 0.4 convolution_add_fusion
  107.5 3.8 %collective-permute-done.7 = f32[256,384]{1,0:T(8,128)S(1)} collective-permute-done((f32[256,384]{1,0:T(8,128)S(1)}, f32[256,384]{1,0:T(8,128)S(1)}, u32[]{:S(2)}, u32[]{:S(2)}) %collective-permute-start.7) | collective-permute-done | bytes 393248 | tf_op jit(solution)/shard_map/ppermute | solution.py:19
  111.4 0.4 convolution_add_fusion.4
  111.7 1.1 maximum_bitcast_fusion
  (9 shorter events, 0.1 us)
Async XLA Ops:
  0.0 16.1 %copy-start.1 = (f32[4,1,1,256,512]{4,3,2,1,0:T(8,128)S(1)}, f32[4,1,1,256,512]{4,3,2,1,0:T(8,128)}, u32[]{:S(2)}) copy-start(f32[4,1,1,256,512]{4,3,2,1,0:T(8,128)} %param.3) | copy-start | bytes 6291460
  2.2 34.5 %collective-permute-start.8 = (f32[256,384]{1,0:T(8,128)}, f32[256,384]{1,0:T(8,128)}, u32[]{:S(2)}, u32[]{:S(2)}) collective-permute-start(f32[256,384]{1,0:T(8,128)} %get-tuple-element.10), channel_id=1, source_target_pairs={{0,256},{16,272},{32,288},{48,304},{64,320},{80,336},{96,352},{112... | collective-permute-start | bytes 1179656 | tf_op jit(solution)/shard_map/ppermute | solution.py:19
  7.1 33.3 %collective-permute-start.4 = (f32[256,384]{1,0:T(8,128)}, f32[256,384]{1,0:T(8,128)}, u32[]{:S(2)}, u32[]{:S(2)}) collective-permute-start(f32[256,384]{1,0:T(8,128)} %get-tuple-element.9), channel_id=1, source_target_pairs={{0,256},{16,272},{32,288},{48,304},{64,320},{80,336},{96,352},{112... | collective-permute-start | bytes 1179656 | tf_op jit(solution)/shard_map/ppermute | solution.py:19
  11.2 19.6 %collective-permute-start = (f32[256,256]{1,0:T(8,128)}, f32[256,256]{1,0:T(8,128)}, u32[]{:S(2)}, u32[]{:S(2)}) collective-permute-start(f32[256,256]{1,0:T(8,128)} %slice.28), channel_id=1, source_target_pairs={{0,256},{16,272},{32,288},{48,304},{64,320},{80,336},{96,352},{112... | collective-permute-start | bytes 786440 | tf_op jit(solution)/shard_map/ppermute | solution.py:19
  16.1 1.2 %copy-start = (f32[1,1,256,1024]{3,2,1,0:T(8,128)S(1)}, f32[1,1,256,1024]{3,2,1,0:T(8,128)}, u32[]{:S(2)}) copy-start(f32[1,1,256,1024]{3,2,1,0:T(8,128)} %param.2) | copy-start | bytes 3145732
  32.1 10.6 %collective-permute-start.1 = (f32[256,256]{1,0:T(8,128)S(1)}, f32[256,256]{1,0:T(8,128)S(1)}, u32[]{:S(2)}, u32[]{:S(2)}) collective-permute-start(f32[256,256]{1,0:T(8,128)S(1)} %convolution_add_fusion.11), channel_id=1, source_target_pairs={{0,8},{1,9},{2,10},{3,11},{4,12},{5,13},{6,14},{7,15},{8,0},{9,1},... | collective-permute-start | bytes 786440 | tf_op jit(solution)/shard_map/ppermute | solution.py:19
  38.5 21.4 %collective-permute-start.9 = (f32[256,384]{1,0:T(8,128)S(1)}, f32[256,384]{1,0:T(8,128)S(1)}, u32[]{:S(2)}, u32[]{:S(2)}) collective-permute-start(f32[256,384]{1,0:T(8,128)S(1)} %convolution_add_fusion.3), channel_id=1, source_target_pairs={{0,8},{1,9},{2,10},{3,11},{4,12},{5,13},{6,14},{7,15},{8,0},{9,1},... | collective-permute-start | bytes 1179656 | tf_op jit(solution)/shard_map/ppermute | solution.py:19
  43.0 8.5 %collective-permute-start.2 = (f32[256,256]{1,0:T(8,128)S(1)}, f32[256,256]{1,0:T(8,128)S(1)}, u32[]{:S(2)}, u32[]{:S(2)}) collective-permute-start(f32[256,256]{1,0:T(8,128)S(1)} %convolution_add_fusion.10), channel_id=1, source_target_pairs={{0,128},{16,144},{32,160},{48,176},{64,192},{80,208},{96,224},{112... | collective-permute-start | bytes 786440 | tf_op jit(solution)/shard_map/ppermute | solution.py:19
  46.7 17.1 %collective-permute-start.5 = (f32[256,384]{1,0:T(8,128)S(1)}, f32[256,384]{1,0:T(8,128)S(1)}, u32[]{:S(2)}, u32[]{:S(2)}) collective-permute-start(f32[256,384]{1,0:T(8,128)S(1)} %convolution_add_fusion.7), channel_id=1, source_target_pairs={{0,8},{1,9},{2,10},{3,11},{4,12},{5,13},{6,14},{7,15},{8,0},{9,1},... | collective-permute-start | bytes 1179656 | tf_op jit(solution)/shard_map/ppermute | solution.py:19
  51.7 15.9 %collective-permute-start.3 = (f32[256,256]{1,0:T(8,128)S(1)}, f32[256,256]{1,0:T(8,128)S(1)}, u32[]{:S(2)}, u32[]{:S(2)}) collective-permute-start(f32[256,256]{1,0:T(8,128)S(1)} %convolution_add_fusion.9), channel_id=1, source_target_pairs={{0,4},{1,5},{2,6},{3,7},{4,0},{5,1},{6,2},{7,3},{8,12},{9,13},{10,... | collective-permute-start | bytes 786440 | tf_op jit(solution)/shard_map/ppermute | solution.py:19
  60.3 13.7 %collective-permute-start.10 = (f32[256,384]{1,0:T(8,128)S(1)}, f32[256,384]{1,0:T(8,128)}, u32[]{:S(2)}, u32[]{:S(2)}) collective-permute-start(f32[256,384]{1,0:T(8,128)S(1)} %convolution_add_fusion.2), channel_id=1, source_target_pairs={{0,128},{16,144},{32,160},{48,176},{64,192},{80,208},{96,224},{112... | collective-permute-start | bytes 1179656 | tf_op jit(solution)/shard_map/ppermute | solution.py:19
  64.2 14.0 %collective-permute-start.6 = (f32[256,384]{1,0:T(8,128)S(1)}, f32[256,384]{1,0:T(8,128)}, u32[]{:S(2)}, u32[]{:S(2)}) collective-permute-start(f32[256,384]{1,0:T(8,128)S(1)} %convolution_add_fusion.6), channel_id=1, source_target_pairs={{0,128},{16,144},{32,160},{48,176},{64,192},{80,208},{96,224},{112... | collective-permute-start | bytes 1179656 | tf_op jit(solution)/shard_map/ppermute | solution.py:19
  75.4 31.7 %collective-permute-start.11 = (f32[256,384]{1,0:T(8,128)S(1)}, f32[256,384]{1,0:T(8,128)S(1)}, u32[]{:S(2)}, u32[]{:S(2)}) collective-permute-start(f32[256,384]{1,0:T(8,128)S(1)} %convolution_add_fusion.1), channel_id=1, source_target_pairs={{0,4},{1,5},{2,6},{3,7},{4,0},{5,1},{6,2},{7,3},{8,12},{9,13},{10,... | collective-permute-start | bytes 1179656 | tf_op jit(solution)/shard_map/ppermute | solution.py:19
  79.6 31.8 %collective-permute-start.7 = (f32[256,384]{1,0:T(8,128)S(1)}, f32[256,384]{1,0:T(8,128)S(1)}, u32[]{:S(2)}, u32[]{:S(2)}) collective-permute-start(f32[256,384]{1,0:T(8,128)S(1)} %convolution_add_fusion.5), channel_id=1, source_target_pairs={{0,4},{1,5},{2,6},{3,7},{4,0},{5,1},{6,2},{7,3},{8,12},{9,13},{10,... | collective-permute-start | bytes 1179656 | tf_op jit(solution)/shard_map/ppermute | solution.py:19

commit v2 on v1

v2 whole, which is shorter than its diff:
```python
import functools

import jax
import jax.numpy as jnp
from jax import lax
from jax.experimental import pallas as pl
from jax.experimental.pallas import tpu as pltpu
from jax.sharding import PartitionSpec as P


WIDTHS = (2, 2, 3, 1)
ORDER = (
    ("s", 0, 0), ("o", 0, 0), ("s", 0, 1), ("d", 0, 0),
    ("s", 1, 0), ("o", 1, 0), ("s", 0, 2), ("o", 0, 1),
    ("d", 0, 1), ("s", 1, 1), ("o", 1, 1), ("d", 1, 0),
    ("s", 2, 0), ("o", 2, 0), ("o", 0, 2), ("d", 0, 2),
    ("s", 1, 2), ("o", 1, 2), ("d", 1, 1), ("s", 2, 1),
    ("o", 2, 1), ("d", 2, 0), ("s", 3, 0), ("o", 3, 0),
    ("d", 1, 2), ("s", 2, 2), ("o", 2, 2), ("d", 2, 1),
    ("s", 3, 1), ("o", 3, 1), ("s", 0, 3), ("o", 0, 3),
    ("d", 2, 2), ("s", 3, 2), ("o", 3, 2), ("d", 0, 3),
    ("s", 1, 3), ("o", 1, 3), ("d", 1, 3), ("s", 2, 3),
    ("o", 2, 3), ("d", 2, 3), ("s", 3, 3), ("o", 3, 3),
    ("d", 3, 0), ("d", 3, 1), ("d", 3, 2), ("d", 3, 3),
)
LAST = 3

ANY = pl.BlockSpec(memory_space=pl.ANY)
VMEM = pl.BlockSpec(memory_space=pltpu.VMEM)


def plan():
    high_top = lax.axis_size("gx").bit_length() - 2
    low_top = lax.axis_size("gy").bit_length() - 2
    return [("gx", high_top), ("gy", low_top), ("gx", high_top - 1), ("gy", low_top - 1)]


def exchange(block, axis, bit):
    route = [(i, i ^ (1 << bit)) for i in range(lax.axis_size(axis))]
    return lax.ppermute(block, axis, route)


def parts(value):
    high = value.astype(jnp.bfloat16)
    return high, (value - high.astype(jnp.float32)).astype(jnp.bfloat16)


def dot(left, right):
    single = functools.partial(jnp.dot, preferred_element_type=jnp.float32)
    left_high, left_low = parts(left)
    right_high, right_low = parts(right)
    return (single(left_low, right_high) + single(left_high, right_low)) + single(left_high, right_high)


def call(kernel, **options):
    params = pltpu.CompilerParams(vmem_limit_bytes=4 << 20)
    return pl.pallas_call(kernel, compiler_params=params, **options)


def cost(shape):
    rank, width = shape
    return pl.CostEstimate(
        flops=6 * rank * rank * width, bytes_accessed=8 * rank * width, transcendentals=0
    )


def half(blocks_ref, level, mine, rank):
    axis, bit = plan()[level]
    upper = jnp.bitwise_and(jnp.right_shift(lax.axis_index(axis), bit), 1)
    start = pl.multiple_of((upper if mine else 1 - upper) * rank, rank)
    return blocks_ref[level, 0, 0, :, pl.ds(start, rank)]


def own_product(level, blocks, here):
    rank = here.shape[0]

    def kernel(blocks_ref, here_ref, out_ref):
        out_ref[...] = dot(half(blocks_ref, level, True, rank), here_ref[...])

    return call(
        kernel,
        out_shape=jax.ShapeDtypeStruct(here.shape, here.dtype),
        in_specs=[VMEM, VMEM],
        out_specs=VMEM,
        cost_estimate=cost(here.shape),
        name="own",
    )(blocks, here)


def add_product(level, blocks, there, own):
    rank = there.shape[0]

    def kernel(blocks_ref, there_ref, own_ref, out_ref):
        block = half(blocks_ref, level, False, rank)
        out_ref[...] = own_ref[...] + dot(block, there_ref[...])

    return call(
        kernel,
        out_shape=jax.ShapeDtypeStruct(there.shape, there.dtype),
        in_specs=[VMEM, VMEM, VMEM],
        out_specs=VMEM,
        cost_estimate=cost(there.shape),
        name="add",
    )(blocks, there, own)


def add_in_place(level, blocks, there, own, whole, span, shape):
    rank = there.shape[0]
    a, b = span

    def kernel(blocks_ref, there_ref, own_ref, *refs):
        out_ref, sum_ref, sem = refs[-3:]
        block = half(blocks_ref, level, False, rank)
        sum_ref[...] = own_ref[...] + dot(block, there_ref[...])
        copy = pltpu.make_async_copy(sum_ref, out_ref.at[0, 0, :, a:b], sem)
        copy.start()
        copy.wait()

    operands = [blocks, there, own] + ([] if whole is None else [whole])
    return call(
        kernel,
        out_shape=jax.ShapeDtypeStruct(shape, there.dtype),
        in_specs=[VMEM, VMEM, VMEM, ANY][: len(operands)],
        out_specs=ANY,
        input_output_aliases={} if whole is None else {3: 0},
        scratch_shapes=[pltpu.VMEM(there.shape, there.dtype), pltpu.SemaphoreType.DMA],
        cost_estimate=cost(there.shape),
        name="finish",
    )(*operands)


def split(state, spans):
    def kernel(source, *refs):
        outs, sems = refs[:-1], refs[-1]
        copies = [
            pltpu.make_async_copy(source.at[:, a:b], out, sems.at[i])
            for i, ((a, b), out) in enumerate(zip(spans, outs))
        ]
        for copy in copies:
            copy.start()
        for copy in copies:
            copy.wait()

    return pl.pallas_call(
        kernel,
        out_shape=[jax.ShapeDtypeStruct((state.shape[0], b - a), state.dtype) for a, b in spans],
        compiler_params=pltpu.CompilerParams(vmem_limit_bytes=4 << 20),
        in_specs=[ANY],
        out_specs=[ANY] * len(spans),
        scratch_shapes=[pltpu.SemaphoreType.DMA((len(spans),))],
        name="split",
    )(state)


def on_device(coefficients, transfer_blocks):
    state = coefficients[0, 0]
    columns = state.shape[1]
    edges = [0]
    for width in WIDTHS:
        edges.append(edges[-1] + width * (columns // 8))
    spans = list(zip(edges, edges[1:]))
    levels = plan()
    pieces = list(split(state, spans))
    arrived, owns = {}, {}
    result = None
    for what, level, piece in ORDER:
        if what == "s":
            arrived[level, piece] = exchange(pieces[piece], *levels[level])
            continue
        if what == "o":
            owns[level, piece] = own_product(level, transfer_blocks, pieces[piece])
            continue
        there, own = arrived[level, piece], owns[level, piece]
        if level < LAST:
            pieces[piece] = add_product(level, transfer_blocks, there, own)
        else:
            result = add_in_place(
                level, transfer_blocks, there, own, result, spans[piece], coefficients.shape
            )
    return result


def solution(mesh):
    in_specs = (P("gx", "gy", None, None), P(None, "gx", "gy", None, None))
    out_specs = P("gx", "gy", None, None)
    return jax.shard_map(
        on_device, mesh=mesh, in_specs=in_specs, out_specs=out_specs, check_vma=False
    )
```

time: 114 us -> 112 us (0.982)
  starting transfers between devices: 49.2 us -> 66.1 us
  matrix products: 14.3 us -> 0 us
  waiting for transfers between devices: 42.7 us -> 29.1 us
  Pallas kernels: 0 us -> 12.5 us
  local copies, waits for them, and re-layouts: 5.18 us -> 2.81 us
    ppermute x12 -> x16, starting transfers between devices: 49.2 us -> 66.1 us  [exchange(): return lax.ppermute(block, axis, route)]
    dot_general x24 -> x0, matrix products: 14.3 us -> none  [dot(): jnp.dot(left, right, preferred_element_type=jnp.float32, precision=lax.Pr...]
    ppermute x12 -> x16, waiting for transfers between devices: 42.7 us -> 29.1 us  [exchange(): return lax.ppermute(block, axis, route)]
    pallas_call x0 -> x33, Pallas kernels: none -> 12.5 us  [the longest x16 4.72 us: own_product(): call(kernel, out_shape=jax.ShapeDtypeStruct(here.shape, here.dtype), in_s...]
    slice x3 -> x0, local copies, waits for them, and re-layouts: 4.02 us -> none  [the longest x2 3.85 us: on_device(): pieces = [state[:, a:b] for a, b in zip(edges, edges[1:])]]
    unnamed x4 -> x6, local copies, waits for them, and re-layouts: 1.03 us -> 2.81 us
  transfers between devices with their start and end apart: 12 -> 16, of which waited for: 7 -> 7; matrix products, arithmetic and copies ran while one was open for 14% -> 0% of each run, Pallas kernels for 0% -> 10%
where the time goes in v2:
time: 112 us; the launch traced here: 111 us
  starting transfers between devices  66.1 us (59%)
  waiting for transfers between devices  29.1 us (26%)
  Pallas kernels  12.5 us (11%)
  local copies, waits for them, and re-layouts  2.81 us (3%)
    ppermute x16, starting transfers between devices, exchange(): return lax.ppermute(block, axis, route)  66.1 us
    ppermute x16, waiting for transfers between devices, exchange(): return lax.ppermute(block, axis, route)  29.1 us
    pallas_call x16, Pallas kernels, own_product(): call(kernel, out_shape=jax.ShapeDtypeStruct(here.shape, here.dtype), in_s...  4.72 us
    pallas_call x4, Pallas kernels, add_in_place(): call(kernel, out_shape=jax.ShapeDtypeStruct(shape, there.dtype), in_specs...  4.05 us
    pallas_call x12, Pallas kernels, add_product(): call(kernel, out_shape=jax.ShapeDtypeStruct(there.shape, there.dtype), in...  3.57 us
    unnamed x6, local copies, waits for them, and re-layouts  2.81 us
  transfers between devices with their start and end apart: 16, of which 7 were waited for; matrix products, arithmetic and copies ran while one was open for 0% of the time, Pallas kernels for 10%

profile of v2, /device:TPU:128, one launch (start us, length us, event | category | flops | bytes accessed | tf_op | source)
XLA Modules:
  0.0 110.9 jit_solution(1751121606730590903)
XLA Ops:
  0.0 1.2 %copy-done.2 = f32[1,1,256,1024]{3,2,1,0:T(8,128)S(1)} copy-done((f32[1,1,256,1024]{3,2,1,0:T(8,128)S(1)}, f32[1,1,256,1024]{3,2,1,0:T(8,128)}, u32[]{:S(2)}) %copy-start.2) | copy-done | bytes 1048600
  1.4 4.9 %collective-permute-start.4 = (f32[256,384]{1,0:T(8,128)S(1)}, f32[256,384]{1,0:T(8,128)S(1)}, u32[]{:S(2)}, u32[]{:S(2)}) collective-permute-start(f32[256,384]{1,0:T(8,128)S(1)} %get-tuple-element.10.here_ref), channel_id=1, source_target_pairs={{0,256},{16,272},{32,288},{48,304},{64,320},{80,336},{96,352},{112... | collective-permute-start | bytes 1179656 | tf_op jit(solution)/shard_map/ppermute | solution.py:40
  6.3 1.6 %copy-done = f32[4,1,1,256,512]{4,3,2,1,0:T(8,128)S(1)} copy-done((f32[4,1,1,256,512]{4,3,2,1,0:T(8,128)S(1)}, f32[4,1,1,256,512]{4,3,2,1,0:T(8,128)}, u32[]{:S(2)}) %copy-start) | copy-done | bytes 2097176
  7.9 0.4 own.20.own_ref
  8.3 7.3 %collective-permute-done.4.there_ref = f32[256,384]{1,0:T(8,128)S(1)} collective-permute-done((f32[256,384]{1,0:T(8,128)S(1)}, f32[256,384]{1,0:T(8,128)S(1)}, u32[]{:S(2)}, u32[]{:S(2)}) %collective-permute-start.4) | collective-permute-done | bytes 393248 | tf_op jit(solution)/shard_map/ppermute | solution.py:40
  15.6 0.4 add.15.here_ref
  16.0 4.3 %collective-permute-start.5 = (f32[256,384]{1,0:T(8,128)S(1)}, f32[256,384]{1,0:T(8,128)S(1)}, u32[]{:S(2)}, u32[]{:S(2)}) collective-permute-start(f32[256,384]{1,0:T(8,128)S(1)} %add.15.here_ref), channel_id=1, source_target_pairs={{0,8},{1,9},{2,10},{3,11},{4,12},{5,13},{6,14},{7,15},{8,0},{9,1},... | collective-permute-start | bytes 1179656 | tf_op jit(solution)/shard_map/ppermute | solution.py:40
  20.3 4.9 %collective-permute-start.12 = (f32[256,256]{1,0:T(8,128)S(1)}, f32[256,256]{1,0:T(8,128)S(1)}, u32[]{:S(2)}, u32[]{:S(2)}) collective-permute-start(f32[256,256]{1,0:T(8,128)S(1)} %get-tuple-element.12.here_ref), channel_id=1, source_target_pairs={{0,256},{16,272},{32,288},{48,304},{64,320},{80,336},{96,352},{112... | collective-permute-start | bytes 786440 | tf_op jit(solution)/shard_map/ppermute | solution.py:40
  25.2 2.4 %collective-permute-start.8 = (f32[256,256]{1,0:T(8,128)S(1)}, f32[256,256]{1,0:T(8,128)S(1)}, u32[]{:S(2)}, u32[]{:S(2)}) collective-permute-start(f32[256,256]{1,0:T(8,128)S(1)} %get-tuple-element.11.here_ref), channel_id=1, source_target_pairs={{0,256},{16,272},{32,288},{48,304},{64,320},{80,336},{96,352},{112... | collective-permute-start | bytes 786440 | tf_op jit(solution)/shard_map/ppermute | solution.py:40
  27.7 0.3 own.28.own_ref
  27.9 0.3 own.24.own_ref
  28.2 3.7 %collective-permute-done.12.there_ref = f32[256,256]{1,0:T(8,128)S(1)} collective-permute-done((f32[256,256]{1,0:T(8,128)S(1)}, f32[256,256]{1,0:T(8,128)S(1)}, u32[]{:S(2)}, u32[]{:S(2)}) %collective-permute-start.12) | collective-permute-done | bytes 262176 | tf_op jit(solution)/shard_map/ppermute | solution.py:40
  31.9 0.3 add.21.here_ref
  32.2 1.9 %collective-permute-start.13 = (f32[256,256]{1,0:T(8,128)S(1)}, f32[256,256]{1,0:T(8,128)S(1)}, u32[]{:S(2)}, u32[]{:S(2)}) collective-permute-start(f32[256,256]{1,0:T(8,128)S(1)} %add.21.here_ref), channel_id=1, source_target_pairs={{0,8},{1,9},{2,10},{3,11},{4,12},{5,13},{6,14},{7,15},{8,0},{9,1},... | collective-permute-start | bytes 786440 | tf_op jit(solution)/shard_map/ppermute | solution.py:40
  34.1 2.1 %collective-permute-done.8.there_ref = f32[256,256]{1,0:T(8,128)S(1)} collective-permute-done((f32[256,256]{1,0:T(8,128)S(1)}, f32[256,256]{1,0:T(8,128)S(1)}, u32[]{:S(2)}, u32[]{:S(2)}) %collective-permute-start.8) | collective-permute-done | bytes 262176 | tf_op jit(solution)/shard_map/ppermute | solution.py:40
  36.2 0.3 add.18.here_ref
  36.5 2.2 %collective-permute-start.9 = (f32[256,256]{1,0:T(8,128)S(1)}, f32[256,256]{1,0:T(8,128)S(1)}, u32[]{:S(2)}, u32[]{:S(2)}) collective-permute-start(f32[256,256]{1,0:T(8,128)S(1)} %add.18.here_ref), channel_id=1, source_target_pairs={{0,8},{1,9},{2,10},{3,11},{4,12},{5,13},{6,14},{7,15},{8,0},{9,1},... | collective-permute-start | bytes 786440 | tf_op jit(solution)/shard_map/ppermute | solution.py:40
  38.7 0.4 own.21.own_ref
  39.1 0.4 add.16.here_ref
  39.5 3.6 %collective-permute-start.6 = (f32[256,384]{1,0:T(8,128)S(1)}, f32[256,384]{1,0:T(8,128)S(1)}, u32[]{:S(2)}, u32[]{:S(2)}) collective-permute-start(f32[256,384]{1,0:T(8,128)S(1)} %add.16.here_ref), channel_id=1, source_target_pairs={{0,128},{16,144},{32,160},{48,176},{64,192},{80,208},{96,224},{112... | collective-permute-start | bytes 1179656 | tf_op jit(solution)/shard_map/ppermute | solution.py:40
  43.1 0.3 own.29.own_ref
  43.4 0.3 own.25.own_ref
  43.7 0.3 add.22.here_ref
  44.0 2.5 %collective-permute-start.14 = (f32[256,256]{1,0:T(8,128)S(1)}, f32[256,256]{1,0:T(8,128)S(1)}, u32[]{:S(2)}, u32[]{:S(2)}) collective-permute-start(f32[256,256]{1,0:T(8,128)S(1)} %add.22.here_ref), channel_id=1, source_target_pairs={{0,128},{16,144},{32,160},{48,176},{64,192},{80,208},{96,224},{112... | collective-permute-start | bytes 786440 | tf_op jit(solution)/shard_map/ppermute | solution.py:40
  46.5 0.3 add.19.here_ref
  46.8 3.6 %collective-permute-start.10 = (f32[256,256]{1,0:T(8,128)S(1)}, f32[256,256]{1,0:T(8,128)S(1)}, u32[]{:S(2)}, u32[]{:S(2)}) collective-permute-start(f32[256,256]{1,0:T(8,128)S(1)} %add.19.here_ref), channel_id=1, source_target_pairs={{0,128},{16,144},{32,160},{48,176},{64,192},{80,208},{96,224},{112... | collective-permute-start | bytes 786440 | tf_op jit(solution)/shard_map/ppermute | solution.py:40
  50.3 5.1 %collective-permute-start = (f32[256,128]{1,0:T(8,128)S(1)}, f32[256,128]{1,0:T(8,128)S(1)}, u32[]{:S(2)}, u32[]{:S(2)}) collective-permute-start(f32[256,128]{1,0:T(8,128)S(1)} %get-tuple-element.9.here_ref), channel_id=1, source_target_pairs={{0,256},{16,272},{32,288},{48,304},{64,320},{80,336},{96,352},{112... | collective-permute-start | bytes 393224 | tf_op jit(solution)/shard_map/ppermute | solution.py:40
  55.7 0.4 own.22.own_ref
  56.1 0.4 add.17.here_ref
  56.4 7.7 %collective-permute-start.7 = (f32[256,384]{1,0:T(8,128)S(1)}, f32[256,384]{1,0:T(8,128)S(1)}, u32[]{:S(2)}, u32[]{:S(2)}) collective-permute-start(f32[256,384]{1,0:T(8,128)S(1)} %add.17.here_ref), channel_id=1, source_target_pairs={{0,4},{1,5},{2,6},{3,7},{4,0},{5,1},{6,2},{7,3},{8,12},{9,13},{10,... | collective-permute-start | bytes 1179656 | tf_op jit(solution)/shard_map/ppermute | solution.py:40
  64.2 2.3 %collective-permute-done.there_ref = f32[256,128]{1,0:T(8,128)S(1)} collective-permute-done((f32[256,128]{1,0:T(8,128)S(1)}, f32[256,128]{1,0:T(8,128)S(1)}, u32[]{:S(2)}, u32[]{:S(2)}) %collective-permute-start) | collective-permute-done | bytes 131104 | tf_op jit(solution)/shard_map/ppermute | solution.py:40
  66.7 3.4 %collective-permute-start.1 = (f32[256,128]{1,0:T(8,128)S(1)}, f32[256,128]{1,0:T(8,128)S(1)}, u32[]{:S(2)}, u32[]{:S(2)}) collective-permute-start(f32[256,128]{1,0:T(8,128)S(1)} %add.12.here_ref), channel_id=1, source_target_pairs={{0,8},{1,9},{2,10},{3,11},{4,12},{5,13},{6,14},{7,15},{8,0},{9,1},... | collective-permute-start | bytes 393224 | tf_op jit(solution)/shard_map/ppermute | solution.py:40
  70.1 0.3 own.30.own_ref
  70.7 0.3 add.23.here_ref
  71.0 7.7 %collective-permute-start.15 = (f32[256,256]{1,0:T(8,128)S(1)}, f32[256,256]{1,0:T(8,128)S(1)}, u32[]{:S(2)}, u32[]{:S(2)}) collective-permute-start(f32[256,256]{1,0:T(8,128)S(1)} %add.23.here_ref), channel_id=1, source_target_pairs={{0,4},{1,5},{2,6},{3,7},{4,0},{5,1},{6,2},{7,3},{8,12},{9,13},{10,... | collective-permute-start | bytes 786440 | tf_op jit(solution)/shard_map/ppermute | solution.py:40
  78.7 0.3 add.20.here_ref
  79.0 2.0 %collective-permute-start.11 = (f32[256,256]{1,0:T(8,128)S(1)}, f32[256,256]{1,0:T(8,128)S(1)}, u32[]{:S(2)}, u32[]{:S(2)}) collective-permute-start(f32[256,256]{1,0:T(8,128)S(1)} %add.20.here_ref), channel_id=1, source_target_pairs={{0,4},{1,5},{2,6},{3,7},{4,0},{5,1},{6,2},{7,3},{8,12},{9,13},{10,... | collective-permute-start | bytes 786440 | tf_op jit(solution)/shard_map/ppermute | solution.py:40
  81.6 2.1 %collective-permute-start.2 = (f32[256,128]{1,0:T(8,128)S(1)}, f32[256,128]{1,0:T(8,128)S(1)}, u32[]{:S(2)}, u32[]{:S(2)}) collective-permute-start(f32[256,128]{1,0:T(8,128)S(1)} %add.13.here_ref), channel_id=1, source_target_pairs={{0,128},{16,144},{32,160},{48,176},{64,192},{80,208},{96,224},{112... | collective-permute-start | bytes 393224 | tf_op jit(solution)/shard_map/ppermute | solution.py:40
  84.0 4.5 %collective-permute-done.2.there_ref = f32[256,128]{1,0:T(8,128)S(1)} collective-permute-done((f32[256,128]{1,0:T(8,128)S(1)}, f32[256,128]{1,0:T(8,128)S(1)}, u32[]{:S(2)}, u32[]{:S(2)}) %collective-permute-start.2) | collective-permute-done | bytes 131104 | tf_op jit(solution)/shard_map/ppermute | solution.py:40
  88.7 7.7 %collective-permute-start.3 = (f32[256,128]{1,0:T(8,128)S(1)}, f32[256,128]{1,0:T(8,128)S(1)}, u32[]{:S(2)}, u32[]{:S(2)}) collective-permute-start(f32[256,128]{1,0:T(8,128)S(1)} %add.14.here_ref), channel_id=1, source_target_pairs={{0,4},{1,5},{2,6},{3,7},{4,0},{5,1},{6,2},{7,3},{8,12},{9,13},{10,... | collective-permute-start | bytes 393224 | tf_op jit(solution)/shard_map/ppermute | solution.py:40
  97.0 0.3 own.27.own_ref
  97.3 2.3 %collective-permute-done.15.there_ref = f32[256,256]{1,0:T(8,128)S(1)} collective-permute-done((f32[256,256]{1,0:T(8,128)S(1)}, f32[256,256]{1,0:T(8,128)S(1)}, u32[]{:S(2)}, u32[]{:S(2)}) %collective-permute-start.15) | collective-permute-done | bytes 262176 | tf_op jit(solution)/shard_map/ppermute | solution.py:40
  99.6 1.0 finish.4.refs_0_
  100.6 6.9 %collective-permute-done.11.there_ref = f32[256,256]{1,0:T(8,128)S(1)} collective-permute-done((f32[256,256]{1,0:T(8,128)S(1)}, f32[256,256]{1,0:T(8,128)S(1)}, u32[]{:S(2)}, u32[]{:S(2)}) %collective-permute-start.11) | collective-permute-done | bytes 262176 | tf_op jit(solution)/shard_map/ppermute | solution.py:40
  107.5 1.0 finish.5.refs_0_
  108.5 0.4 own.23.own_ref
  108.8 1.1 %finish.6.refs_0_ = f32[1,1,256,1024]{3,2,1,0:T(8,128)} custom-call(f32[4,1,1,256,512]{4,3,2,1,0:T(8,128)S(1)} %copy-done.1, f32[256,384]{1,0:T(8,128)S(1)} %collective-permute-done.7.there_ref, f32[256,384]{1,0:T(8,128)S(1)} %own.23.own_ref, f32[1,1,256,1024]{3,2,1,0:T(8,128)} %finish.5.refs_0_), custom_call_target="tpu_custom_call", output_to_operand_aliasing={{}: (3, {})} | custom-call | flops 150994944 | bytes 786432 | tf_op jit(solution)/shard_map/finish/pallas_call | solution.py:120
  110.0 0.9 finish.7
  (23 shorter events, 2.5 us)
Async XLA Ops:
  0.0 1.2 %copy-start.2 = (f32[1,1,256,1024]{3,2,1,0:T(8,128)S(1)}, f32[1,1,256,1024]{3,2,1,0:T(8,128)}, u32[]{:S(2)}) copy-start(f32[1,1,256,1024]{3,2,1,0:T(8,128)} %param.2) | copy-start | bytes 3145732
  1.4 14.3 %collective-permute-start.4 = (f32[256,384]{1,0:T(8,128)S(1)}, f32[256,384]{1,0:T(8,128)S(1)}, u32[]{:S(2)}, u32[]{:S(2)}) collective-permute-start(f32[256,384]{1,0:T(8,128)S(1)} %get-tuple-element.10.here_ref), channel_id=1, source_target_pairs={{0,256},{16,272},{32,288},{48,304},{64,320},{80,336},{96,352},{112... | collective-permute-start | bytes 1179656 | tf_op jit(solution)/shard_map/ppermute | solution.py:40
  6.3 1.6 %copy-start = (f32[4,1,1,256,512]{4,3,2,1,0:T(8,128)S(1)}, f32[4,1,1,256,512]{4,3,2,1,0:T(8,128)}, u32[]{:S(2)}) copy-start(f32[4,1,1,256,512]{4,3,2,1,0:T(8,128)} %blocks_ref.63) | copy-start | bytes 6291460
  7.9 7.7 %copy-start.1 = (f32[4,1,1,256,512]{4,3,2,1,0:T(8,128)S(1)}, f32[4,1,1,256,512]{4,3,2,1,0:T(8,128)}, u32[]{:S(2)}) copy-start(f32[4,1,1,256,512]{4,3,2,1,0:T(8,128)} %blocks_ref.63) | copy-start | bytes 6291460
  16.0 23.1 %collective-permute-start.5 = (f32[256,384]{1,0:T(8,128)S(1)}, f32[256,384]{1,0:T(8,128)S(1)}, u32[]{:S(2)}, u32[]{:S(2)}) collective-permute-start(f32[256,384]{1,0:T(8,128)S(1)} %add.15.here_ref), channel_id=1, source_target_pairs={{0,8},{1,9},{2,10},{3,11},{4,12},{5,13},{6,14},{7,15},{8,0},{9,1},... | collective-permute-start | bytes 1179656 | tf_op jit(solution)/shard_map/ppermute | solution.py:40
  20.3 11.6 %collective-permute-start.12 = (f32[256,256]{1,0:T(8,128)S(1)}, f32[256,256]{1,0:T(8,128)S(1)}, u32[]{:S(2)}, u32[]{:S(2)}) collective-permute-start(f32[256,256]{1,0:T(8,128)S(1)} %get-tuple-element.12.here_ref), channel_id=1, source_target_pairs={{0,256},{16,272},{32,288},{48,304},{64,320},{80,336},{96,352},{112... | collective-permute-start | bytes 786440 | tf_op jit(solution)/shard_map/ppermute | solution.py:40
  25.2 11.0 %collective-permute-start.8 = (f32[256,256]{1,0:T(8,128)S(1)}, f32[256,256]{1,0:T(8,128)S(1)}, u32[]{:S(2)}, u32[]{:S(2)}) collective-permute-start(f32[256,256]{1,0:T(8,128)S(1)} %get-tuple-element.11.here_ref), channel_id=1, source_target_pairs={{0,256},{16,272},{32,288},{48,304},{64,320},{80,336},{96,352},{112... | collective-permute-start | bytes 786440 | tf_op jit(solution)/shard_map/ppermute | solution.py:40
  32.2 11.4 %collective-permute-start.13 = (f32[256,256]{1,0:T(8,128)S(1)}, f32[256,256]{1,0:T(8,128)S(1)}, u32[]{:S(2)}, u32[]{:S(2)}) collective-permute-start(f32[256,256]{1,0:T(8,128)S(1)} %add.21.here_ref), channel_id=1, source_target_pairs={{0,8},{1,9},{2,10},{3,11},{4,12},{5,13},{6,14},{7,15},{8,0},{9,1},... | collective-permute-start | bytes 786440 | tf_op jit(solution)/shard_map/ppermute | solution.py:40
  36.5 10.0 %collective-permute-start.9 = (f32[256,256]{1,0:T(8,128)S(1)}, f32[256,256]{1,0:T(8,128)S(1)}, u32[]{:S(2)}, u32[]{:S(2)}) collective-permute-start(f32[256,256]{1,0:T(8,128)S(1)} %add.18.here_ref), channel_id=1, source_target_pairs={{0,8},{1,9},{2,10},{3,11},{4,12},{5,13},{6,14},{7,15},{8,0},{9,1},... | collective-permute-start | bytes 786440 | tf_op jit(solution)/shard_map/ppermute | solution.py:40
  39.5 16.6 %collective-permute-start.6 = (f32[256,384]{1,0:T(8,128)S(1)}, f32[256,384]{1,0:T(8,128)S(1)}, u32[]{:S(2)}, u32[]{:S(2)}) collective-permute-start(f32[256,384]{1,0:T(8,128)S(1)} %add.16.here_ref), channel_id=1, source_target_pairs={{0,128},{16,144},{32,160},{48,176},{64,192},{80,208},{96,224},{112... | collective-permute-start | bytes 1179656 | tf_op jit(solution)/shard_map/ppermute | solution.py:40
  44.0 26.7 %collective-permute-start.14 = (f32[256,256]{1,0:T(8,128)S(1)}, f32[256,256]{1,0:T(8,128)S(1)}, u32[]{:S(2)}, u32[]{:S(2)}) collective-permute-start(f32[256,256]{1,0:T(8,128)S(1)} %add.22.here_ref), channel_id=1, source_target_pairs={{0,128},{16,144},{32,160},{48,176},{64,192},{80,208},{96,224},{112... | collective-permute-start | bytes 786440 | tf_op jit(solution)/shard_map/ppermute | solution.py:40
  46.8 32.0 %collective-permute-start.10 = (f32[256,256]{1,0:T(8,128)S(1)}, f32[256,256]{1,0:T(8,128)S(1)}, u32[]{:S(2)}, u32[]{:S(2)}) collective-permute-start(f32[256,256]{1,0:T(8,128)S(1)} %add.19.here_ref), channel_id=1, source_target_pairs={{0,128},{16,144},{32,160},{48,176},{64,192},{80,208},{96,224},{112... | collective-permute-start | bytes 786440 | tf_op jit(solution)/shard_map/ppermute | solution.py:40
  50.3 16.2 %collective-permute-start = (f32[256,128]{1,0:T(8,128)S(1)}, f32[256,128]{1,0:T(8,128)S(1)}, u32[]{:S(2)}, u32[]{:S(2)}) collective-permute-start(f32[256,128]{1,0:T(8,128)S(1)} %get-tuple-element.9.here_ref), channel_id=1, source_target_pairs={{0,256},{16,272},{32,288},{48,304},{64,320},{80,336},{96,352},{112... | collective-permute-start | bytes 393224 | tf_op jit(solution)/shard_map/ppermute | solution.py:40
  56.4 52.4 %collective-permute-start.7 = (f32[256,384]{1,0:T(8,128)S(1)}, f32[256,384]{1,0:T(8,128)S(1)}, u32[]{:S(2)}, u32[]{:S(2)}) collective-permute-start(f32[256,384]{1,0:T(8,128)S(1)} %add.17.here_ref), channel_id=1, source_target_pairs={{0,4},{1,5},{2,6},{3,7},{4,0},{5,1},{6,2},{7,3},{8,12},{9,13},{10,... | collective-permute-start | bytes 1179656 | tf_op jit(solution)/shard_map/ppermute | solution.py:40
  66.7 14.6 %collective-permute-start.1 = (f32[256,128]{1,0:T(8,128)S(1)}, f32[256,128]{1,0:T(8,128)S(1)}, u32[]{:S(2)}, u32[]{:S(2)}) collective-permute-start(f32[256,128]{1,0:T(8,128)S(1)} %add.12.here_ref), channel_id=1, source_target_pairs={{0,8},{1,9},{2,10},{3,11},{4,12},{5,13},{6,14},{7,15},{8,0},{9,1},... | collective-permute-start | bytes 393224 | tf_op jit(solution)/shard_map/ppermute | solution.py:40
  71.0 28.6 %collective-permute-start.15 = (f32[256,256]{1,0:T(8,128)S(1)}, f32[256,256]{1,0:T(8,128)S(1)}, u32[]{:S(2)}, u32[]{:S(2)}) collective-permute-start(f32[256,256]{1,0:T(8,128)S(1)} %add.23.here_ref), channel_id=1, source_target_pairs={{0,4},{1,5},{2,6},{3,7},{4,0},{5,1},{6,2},{7,3},{8,12},{9,13},{10,... | collective-permute-start | bytes 786440 | tf_op jit(solution)/shard_map/ppermute | solution.py:40
  79.0 28.4 %collective-permute-start.11 = (f32[256,256]{1,0:T(8,128)S(1)}, f32[256,256]{1,0:T(8,128)S(1)}, u32[]{:S(2)}, u32[]{:S(2)}) collective-permute-start(f32[256,256]{1,0:T(8,128)S(1)} %add.20.here_ref), channel_id=1, source_target_pairs={{0,4},{1,5},{2,6},{3,7},{4,0},{5,1},{6,2},{7,3},{8,12},{9,13},{10,... | collective-permute-start | bytes 786440 | tf_op jit(solution)/shard_map/ppermute | solution.py:40
  81.6 6.9 %collective-permute-start.2 = (f32[256,128]{1,0:T(8,128)S(1)}, f32[256,128]{1,0:T(8,128)S(1)}, u32[]{:S(2)}, u32[]{:S(2)}) collective-permute-start(f32[256,128]{1,0:T(8,128)S(1)} %add.13.here_ref), channel_id=1, source_target_pairs={{0,128},{16,144},{32,160},{48,176},{64,192},{80,208},{96,224},{112... | collective-permute-start | bytes 393224 | tf_op jit(solution)/shard_map/ppermute | solution.py:40
  88.7 21.3 %collective-permute-start.3 = (f32[256,128]{1,0:T(8,128)S(1)}, f32[256,128]{1,0:T(8,128)S(1)}, u32[]{:S(2)}, u32[]{:S(2)}) collective-permute-start(f32[256,128]{1,0:T(8,128)S(1)} %add.14.here_ref), channel_id=1, source_target_pairs={{0,4},{1,5},{2,6},{3,7},{4,0},{5,1},{6,2},{7,3},{8,12},{9,13},{10,... | collective-permute-start | bytes 393224 | tf_op jit(solution)/shard_map/ppermute | solution.py:40

commit v3 on v2

v3 whole, which is shorter than its diff:
```python
import functools

import jax
import jax.numpy as jnp
from jax import lax
from jax.experimental import pallas as pl
from jax.experimental.pallas import tpu as pltpu
from jax.sharding import PartitionSpec as P


BEGINS = ((0, 2, 4), (0, 2, 4), (0, 2, 4, 6), (0, 2, 4, 6))
ORDER = (
    ("s", 0, 0), ("s", 0, 2), ("s", 0, 4), ("d", 0, 0),
    ("s", 1, 0), ("d", 0, 2), ("s", 1, 2), ("d", 1, 0),
    ("s", 2, 0), ("d", 0, 4), ("s", 1, 4), ("d", 1, 2),
    ("s", 2, 2), ("d", 2, 0), ("s", 3, 0), ("d", 2, 2),
    ("s", 3, 2), ("d", 1, 4), ("s", 2, 4), ("s", 2, 6),
    ("d", 2, 4), ("s", 3, 4), ("d", 2, 6), ("s", 3, 6),
    ("d", 3, 0), ("d", 3, 2), ("d", 3, 4), ("d", 3, 6),
)
LAST = 3
EARLY = ()

ANY = pl.BlockSpec(memory_space=pl.ANY)
VMEM = pl.BlockSpec(memory_space=pltpu.VMEM)


def plan():
    high_top = lax.axis_size("gx").bit_length() - 2
    low_top = lax.axis_size("gy").bit_length() - 2
    return [("gx", high_top), ("gy", low_top), ("gx", high_top - 1), ("gy", low_top - 1)]


def exchange(block, axis, bit):
    route = [(i, i ^ (1 << bit)) for i in range(lax.axis_size(axis))]
    return lax.ppermute(block, axis, route)


def parts(value):
    high = value.astype(jnp.bfloat16)
    return high, (value - high.astype(jnp.float32)).astype(jnp.bfloat16)


def dot(left, right):
    single = functools.partial(jnp.dot, preferred_element_type=jnp.float32)
    left_high, left_low = parts(left)
    right_high, right_low = parts(right)
    return (single(left_low, right_high) + single(left_high, right_low)) + single(left_high, right_high)


def call(kernel, limit=4 << 20, **options):
    params = pltpu.CompilerParams(vmem_limit_bytes=limit)
    return pl.pallas_call(kernel, compiler_params=params, **options)


def cost(shape):
    rank, width = shape
    return pl.CostEstimate(
        flops=12 * rank * rank * width, bytes_accessed=12 * rank * width, transcendentals=0
    )


def products(level, blocks_ref, here, there):
    axis, bit = plan()[level]
    rank = here.shape[0]
    upper = jnp.bitwise_and(jnp.right_shift(lax.axis_index(axis), bit), 1)
    mine = blocks_ref[:, pl.ds(pl.multiple_of(upper * rank, rank), rank)]
    other = blocks_ref[:, pl.ds(pl.multiple_of((1 - upper) * rank, rank), rank)]
    return dot(mine, here) + dot(other, there)


def fetch(level, blocks_ref, held_ref, sem):
    copy = pltpu.make_async_copy(blocks_ref.at[level, 0, 0], held_ref, sem)
    copy.start()
    copy.wait()


def held(blocks):
    return [pltpu.VMEM(blocks.shape[3:], blocks.dtype), pltpu.SemaphoreType.DMA]


def apply(level, blocks, here, there, spans, limit):
    rank = here.shape[0]

    def kernel(blocks_ref, here_ref, there_ref, *refs):
        *outs, held_ref, sem = refs
        fetch(level, blocks_ref, held_ref, sem)
        for (a, b), out in zip(spans, outs):
            out[...] = products(level, held_ref, here_ref[:, a:b], there_ref[:, a:b])

    return call(
        kernel,
        out_shape=[jax.ShapeDtypeStruct((rank, b - a), here.dtype) for a, b in spans],
        in_specs=[ANY, VMEM, VMEM],
        out_specs=[VMEM] * len(spans),
        scratch_shapes=held(blocks),
        cost_estimate=cost(here.shape),
        limit=limit,
        name="apply",
    )(blocks, here, there)


def apply_in_place(level, blocks, here, there, whole, span, shape):
    a, b = span

    def kernel(blocks_ref, here_ref, there_ref, *refs):
        out_ref, sum_ref, held_ref, sem = refs[-4:]
        fetch(level, blocks_ref, held_ref, sem)
        sum_ref[...] = products(level, held_ref, here_ref[...], there_ref[...])
        copy = pltpu.make_async_copy(sum_ref, out_ref.at[0, 0, :, a:b], sem)
        copy.start()
        copy.wait()

    operands = [blocks, here, there] + ([] if whole is None else [whole])
    return call(
        kernel,
        out_shape=jax.ShapeDtypeStruct(shape, here.dtype),
        in_specs=[ANY, VMEM, VMEM, ANY][: len(operands)],
        out_specs=ANY,
        input_output_aliases={} if whole is None else {3: 0},
        scratch_shapes=[pltpu.VMEM(here.shape, here.dtype)] + held(blocks),
        cost_estimate=cost(here.shape),
        name="finish",
    )(*operands)


def split(state, spans):
    def kernel(source, *refs):
        outs, sems = refs[:-1], refs[-1]
        copies = [
            pltpu.make_async_copy(source.at[:, a:b], out, sems.at[i])
            for i, ((a, b), out) in enumerate(zip(spans, outs))
        ]
        for copy in copies:
            copy.start()
        for copy in copies:
            copy.wait()

    return pl.pallas_call(
        kernel,
        out_shape=[jax.ShapeDtypeStruct((state.shape[0], b - a), state.dtype) for a, b in spans],
        compiler_params=pltpu.CompilerParams(vmem_limit_bytes=4 << 20),
        in_specs=[ANY],
        out_specs=[ANY] * len(spans),
        scratch_shapes=[pltpu.SemaphoreType.DMA((len(spans),))],
        cost_estimate=pl.CostEstimate(flops=1 << 36, bytes_accessed=1 << 26, transcendentals=0),
        name="split",
    )(state)


def spans_of(level, columns):
    begins = BEGINS[level]
    ends = begins[1:] + (8,)
    return {a: (a * columns // 8, b * columns // 8) for a, b in zip(begins, ends)}


def on_device(coefficients, transfer_blocks):
    state = coefficients[0, 0]
    columns = state.shape[1]
    levels = plan()
    spans = [spans_of(level, columns) for level in range(len(levels))]
    pieces = [dict() for _ in levels]
    pieces[0] = dict(zip(spans[0], split(state, list(spans[0].values()))))
    arrived = {}
    result = None
    for what, level, piece in ORDER:
        if what == "s":
            arrived[level, piece] = exchange(pieces[level][piece], *levels[level])
            continue
        here, there = pieces[level][piece], arrived[level, piece]
        first, last = spans[level][piece]
        if level == LAST:
            result = apply_in_place(
                level, transfer_blocks, here, there, result, (first, last), coefficients.shape
            )
            continue
        inner = {n: s for n, s in spans[level + 1].items() if first <= s[0] < last}
        within = [(a - first, b - first) for a, b in inner.values()]
        limit = 60 * 1024 * 1024 if (level, piece) in EARLY else 4 << 20
        sums = apply(level, transfer_blocks, here, there, within, limit)
        pieces[level + 1].update(zip(inner, sums))
    return result


def solution(mesh):
    in_specs = (P("gx", "gy", None, None), P(None, "gx", "gy", None, None))
    out_specs = P("gx", "gy", None, None)
    return jax.shard_map(
        on_device, mesh=mesh, in_specs=in_specs, out_specs=out_specs, check_vma=False
    )
```

time: 112 us -> 109 us (0.973)
  the two profiles are of different devices: /device:TPU:128 before, /device:TPU:2 now
where the time goes in v3:
time: 109 us; the launch traced here: 108 us
  starting transfers between devices  56.6 us (52%)
  waiting for transfers between devices  40.6 us (37%)
  Pallas kernels  9.59 us (9%)
  local copies, waits for them, and re-layouts  1.23 us (1%)
    ppermute x14, starting transfers between devices, exchange(): return lax.ppermute(block, axis, route)  56.6 us
    ppermute x14, waiting for transfers between devices, exchange(): return lax.ppermute(block, axis, route)  40.6 us
    pallas_call x10, Pallas kernels, apply(): call(kernel, out_shape=[jax.ShapeDtypeStruct((rank, b - a), here.dtype) f...  4.88 us
    pallas_call x4, Pallas kernels, apply_in_place(): call(kernel, out_shape=jax.ShapeDtypeStruct(shape, here.dtype), in_specs=...  4.59 us
  transfers between devices with their start and end apart: 14, of which 6 were waited for; matrix products, arithmetic and copies ran while one was open for 0% of the time, Pallas kernels for 8%

profile of v3, /device:TPU:2, one launch (start us, length us, event | category | flops | bytes accessed | tf_op | source)
XLA Modules:
  0.0 108.3 jit_solution(914523010776661774)
XLA Ops:
  0.0 0.0 copy-start.1
  0.0 1.2 %copy-done.1 = f32[1,1,256,1024]{3,2,1,0:T(8,128)S(1)} copy-done((f32[1,1,256,1024]{3,2,1,0:T(8,128)S(1)}, f32[1,1,256,1024]{3,2,1,0:T(8,128)}, u32[]{:S(2)}) %copy-start.1) | copy-done | bytes 1048600
  1.2 0.0 copy-start
  1.2 0.1 split.1
  1.4 4.2 %collective-permute-start = (f32[256,512]{1,0:T(8,128)S(1)}, f32[256,512]{1,0:T(8,128)S(1)}, u32[]{:S(2)}, u32[]{:S(2)}) collective-permute-start(f32[256,512]{1,0:T(8,128)S(1)} %get-tuple-element.10.here_ref), channel_id=1, source_target_pairs={{0,256},{16,272},{32,288},{48,304},{64,320},{80,336},{96,352},{112... | collective-permute-start | bytes 1572872 | tf_op jit(solution)/shard_map/ppermute | solution.py:36
  5.5 3.3 %collective-permute-start.10 = (f32[256,256]{1,0:T(8,128)S(1)}, f32[256,256]{1,0:T(8,128)S(1)}, u32[]{:S(2)}, u32[]{:S(2)}) collective-permute-start(f32[256,256]{1,0:T(8,128)S(1)} %get-tuple-element.14.here_ref), channel_id=1, source_target_pairs={{0,256},{16,272},{32,288},{48,304},{64,320},{80,336},{96,352},{112... | collective-permute-start | bytes 786440 | tf_op jit(solution)/shard_map/ppermute | solution.py:36
  8.8 4.0 %collective-permute-start.6 = (f32[256,256]{1,0:T(8,128)S(1)}, f32[256,256]{1,0:T(8,128)S(1)}, u32[]{:S(2)}, u32[]{:S(2)}) collective-permute-start(f32[256,256]{1,0:T(8,128)S(1)} %get-tuple-element.13.here_ref), channel_id=1, source_target_pairs={{0,256},{16,272},{32,288},{48,304},{64,320},{80,336},{96,352},{112... | collective-permute-start | bytes 786440 | tf_op jit(solution)/shard_map/ppermute | solution.py:36
  12.9 6.8 %collective-permute-done.there_ref = f32[256,512]{1,0:T(8,128)S(1)} collective-permute-done((f32[256,512]{1,0:T(8,128)S(1)}, f32[256,512]{1,0:T(8,128)S(1)}, u32[]{:S(2)}, u32[]{:S(2)}) %collective-permute-start) | collective-permute-done | bytes 524320 | tf_op jit(solution)/shard_map/ppermute | solution.py:36
  19.7 0.0 copy-done
  19.7 0.7 apply.10.here_ref
  20.3 4.3 %collective-permute-start.1 = (f32[256,512]{1,0:T(8,128)S(1)}, f32[256,512]{1,0:T(8,128)S(1)}, u32[]{:S(2)}, u32[]{:S(2)}) collective-permute-start(f32[256,512]{1,0:T(8,128)S(1)} %apply.10.here_ref), channel_id=1, source_target_pairs={{0,8},{1,9},{2,10},{3,11},{4,12},{5,13},{6,14},{7,15},{8,0},{9,1},... | collective-permute-start | bytes 1572872 | tf_op jit(solution)/shard_map/ppermute | solution.py:36
  24.6 0.7 collective-permute-done.10.there_ref
  25.3 0.4 apply.17.here_ref
  25.8 4.3 %collective-permute-start.11 = (f32[256,256]{1,0:T(8,128)S(1)}, f32[256,256]{1,0:T(8,128)S(1)}, u32[]{:S(2)}, u32[]{:S(2)}) collective-permute-start(f32[256,256]{1,0:T(8,128)S(1)} %apply.17.here_ref), channel_id=1, source_target_pairs={{0,8},{1,9},{2,10},{3,11},{4,12},{5,13},{6,14},{7,15},{8,0},{9,1},... | collective-permute-start | bytes 786440 | tf_op jit(solution)/shard_map/ppermute | solution.py:36
  30.0 0.0 collective-permute-done.6.there_ref
  30.1 0.5 apply.14.here_ref
  30.5 4.0 %collective-permute-start.7 = (f32[256,256]{1,0:T(8,128)S(1)}, f32[256,256]{1,0:T(8,128)S(1)}, u32[]{:S(2)}, u32[]{:S(2)}) collective-permute-start(f32[256,256]{1,0:T(8,128)S(1)} %apply.14.here_ref), channel_id=1, source_target_pairs={{0,8},{1,9},{2,10},{3,11},{4,12},{5,13},{6,14},{7,15},{8,0},{9,1},... | collective-permute-start | bytes 786440 | tf_op jit(solution)/shard_map/ppermute | solution.py:36
  34.5 8.4 %collective-permute-done.11.there_ref = f32[256,256]{1,0:T(8,128)S(1)} collective-permute-done((f32[256,256]{1,0:T(8,128)S(1)}, f32[256,256]{1,0:T(8,128)S(1)}, u32[]{:S(2)}, u32[]{:S(2)}) %collective-permute-start.11) | collective-permute-done | bytes 262176 | tf_op jit(solution)/shard_map/ppermute | solution.py:36
  43.0 0.4 apply.18.here_ref
  43.4 2.5 %collective-permute-start.12 = (f32[256,256]{1,0:T(8,128)S(1)}, f32[256,256]{1,0:T(8,128)S(1)}, u32[]{:S(2)}, u32[]{:S(2)}) collective-permute-start(f32[256,256]{1,0:T(8,128)S(1)} %apply.18.here_ref), channel_id=1, source_target_pairs={{0,128},{16,144},{32,160},{48,176},{64,192},{80,208},{96,224},{112... | collective-permute-start | bytes 786440 | tf_op jit(solution)/shard_map/ppermute | solution.py:36
  45.9 0.0 collective-permute-done.7.there_ref
  45.9 0.4 apply.15.here_ref
  46.4 3.4 %collective-permute-start.8 = (f32[256,256]{1,0:T(8,128)S(1)}, f32[256,256]{1,0:T(8,128)S(1)}, u32[]{:S(2)}, u32[]{:S(2)}) collective-permute-start(f32[256,256]{1,0:T(8,128)S(1)} %apply.15.here_ref), channel_id=1, source_target_pairs={{0,128},{16,144},{32,160},{48,176},{64,192},{80,208},{96,224},{112... | collective-permute-start | bytes 786440 | tf_op jit(solution)/shard_map/ppermute | solution.py:36
  49.8 0.0 collective-permute-done.1.there_ref
  49.8 0.7 apply.11
  50.4 2.4 %collective-permute-start.4 = (f32[256,256]{1,0:T(8,128)S(1)}, f32[256,256]{1,0:T(8,128)S(1)}, u32[]{:S(2)}, u32[]{:S(2)}) collective-permute-start(f32[256,256]{1,0:T(8,128)S(1)} %get-tuple-element.12.here_ref), channel_id=1, source_target_pairs={{0,128},{16,144},{32,160},{48,176},{64,192},{80,208},{96,224},{112... | collective-permute-start | bytes 786440 | tf_op jit(solution)/shard_map/ppermute | solution.py:36
  52.9 3.4 %collective-permute-start.2 = (f32[256,256]{1,0:T(8,128)S(1)}, f32[256,256]{1,0:T(8,128)S(1)}, u32[]{:S(2)}, u32[]{:S(2)}) collective-permute-start(f32[256,256]{1,0:T(8,128)S(1)} %get-tuple-element.11.here_ref), channel_id=1, source_target_pairs={{0,128},{16,144},{32,160},{48,176},{64,192},{80,208},{96,224},{112... | collective-permute-start | bytes 786440 | tf_op jit(solution)/shard_map/ppermute | solution.py:36
  56.3 0.0 collective-permute-done.12.there_ref
  56.3 0.4 apply.19.here_ref
  56.8 7.7 %collective-permute-start.13 = (f32[256,256]{1,0:T(8,128)S(1)}, f32[256,256]{1,0:T(8,128)S(1)}, u32[]{:S(2)}, u32[]{:S(2)}) collective-permute-start(f32[256,256]{1,0:T(8,128)S(1)} %apply.19.here_ref), channel_id=1, source_target_pairs={{0,4},{1,5},{2,6},{3,7},{4,0},{5,1},{6,2},{7,3},{8,12},{9,13},{10,... | collective-permute-start | bytes 786440 | tf_op jit(solution)/shard_map/ppermute | solution.py:36
  64.5 0.0 collective-permute-done.8.there_ref
  64.5 0.4 apply.16.here_ref
  65.0 3.4 %collective-permute-start.9 = (f32[256,256]{1,0:T(8,128)S(1)}, f32[256,256]{1,0:T(8,128)S(1)}, u32[]{:S(2)}, u32[]{:S(2)}) collective-permute-start(f32[256,256]{1,0:T(8,128)S(1)} %apply.16.here_ref), channel_id=1, source_target_pairs={{0,4},{1,5},{2,6},{3,7},{4,0},{5,1},{6,2},{7,3},{8,12},{9,13},{10,... | collective-permute-start | bytes 786440 | tf_op jit(solution)/shard_map/ppermute | solution.py:36
  68.3 0.0 collective-permute-done.4.there_ref
  68.3 0.4 apply.13.here_ref
  68.8 6.4 %collective-permute-start.5 = (f32[256,256]{1,0:T(8,128)S(1)}, f32[256,256]{1,0:T(8,128)S(1)}, u32[]{:S(2)}, u32[]{:S(2)}) collective-permute-start(f32[256,256]{1,0:T(8,128)S(1)} %apply.13.here_ref), channel_id=1, source_target_pairs={{0,4},{1,5},{2,6},{3,7},{4,0},{5,1},{6,2},{7,3},{8,12},{9,13},{10,... | collective-permute-start | bytes 786440 | tf_op jit(solution)/shard_map/ppermute | solution.py:36
  75.2 0.0 collective-permute-done.2.there_ref
  75.2 0.4 apply.12.here_ref
  75.6 3.4 %collective-permute-start.3 = (f32[256,256]{1,0:T(8,128)S(1)}, f32[256,256]{1,0:T(8,128)S(1)}, u32[]{:S(2)}, u32[]{:S(2)}) collective-permute-start(f32[256,256]{1,0:T(8,128)S(1)} %apply.12.here_ref), channel_id=1, source_target_pairs={{0,4},{1,5},{2,6},{3,7},{4,0},{5,1},{6,2},{7,3},{8,12},{9,13},{10,... | collective-permute-start | bytes 786440 | tf_op jit(solution)/shard_map/ppermute | solution.py:36
  79.0 0.0 collective-permute-done.13.there_ref
  79.0 1.1 %finish.4.refs_0_ = f32[1,1,256,1024]{3,2,1,0:T(8,128)} custom-call(f32[4,1,1,256,512]{4,3,2,1,0:T(8,128)S(1)} %copy-done, f32[256,256]{1,0:T(8,128)S(1)} %apply.19.here_ref, f32[256,256]{1,0:T(8,128)S(1)} %collective-permute-done.13.there_ref), custom_call_target="tpu_custom_call" | custom-call | flops 201326592 | bytes 786432 | tf_op jit(solution)/shard_map/finish/pallas_call | solution.py:115
  80.2 8.4 %collective-permute-done.9.there_ref = f32[256,256]{1,0:T(8,128)S(1)} collective-permute-done((f32[256,256]{1,0:T(8,128)S(1)}, f32[256,256]{1,0:T(8,128)S(1)}, u32[]{:S(2)}, u32[]{:S(2)}) %collective-permute-start.9) | collective-permute-done | bytes 262176 | tf_op jit(solution)/shard_map/ppermute | solution.py:36
  88.6 1.1 %finish.5.refs_0_ = f32[1,1,256,1024]{3,2,1,0:T(8,128)} custom-call(f32[4,1,1,256,512]{4,3,2,1,0:T(8,128)S(1)} %copy-done, f32[256,256]{1,0:T(8,128)S(1)} %apply.16.here_ref, f32[256,256]{1,0:T(8,128)S(1)} %collective-permute-done.9.there_ref, f32[1,1,256,1024]{3,2,1,0:T(8,128)} %finish.4.refs_0_), custom_call_target="tpu_custom_call", output_to_operand_aliasing={{}: (3, {})} | custom-call | flops 201326592 | bytes 786432 | tf_op jit(solution)/shard_map/finish/pallas_call | solution.py:115
  89.8 12.8 %collective-permute-done.5.there_ref = f32[256,256]{1,0:T(8,128)S(1)} collective-permute-done((f32[256,256]{1,0:T(8,128)S(1)}, f32[256,256]{1,0:T(8,128)S(1)}, u32[]{:S(2)}, u32[]{:S(2)}) %collective-permute-start.5) | collective-permute-done | bytes 262176 | tf_op jit(solution)/shard_map/ppermute | solution.py:36
  102.6 1.2 %finish.6.refs_0_ = f32[1,1,256,1024]{3,2,1,0:T(8,128)} custom-call(f32[4,1,1,256,512]{4,3,2,1,0:T(8,128)S(1)} %copy-done, f32[256,256]{1,0:T(8,128)S(1)} %apply.13.here_ref, f32[256,256]{1,0:T(8,128)S(1)} %collective-permute-done.5.there_ref, f32[1,1,256,1024]{3,2,1,0:T(8,128)} %finish.5.refs_0_), custom_call_target="tpu_custom_call", output_to_operand_aliasing={{}: (3, {})} | custom-call | flops 201326592 | bytes 786432 | tf_op jit(solution)/shard_map/finish/pallas_call | solution.py:115
  103.7 3.4 %collective-permute-done.3.there_ref = f32[256,256]{1,0:T(8,128)S(1)} collective-permute-done((f32[256,256]{1,0:T(8,128)S(1)}, f32[256,256]{1,0:T(8,128)S(1)}, u32[]{:S(2)}, u32[]{:S(2)}) %collective-permute-start.3) | collective-permute-done | bytes 262176 | tf_op jit(solution)/shard_map/ppermute | solution.py:36
  107.2 1.1 %finish.7 = f32[1,1,256,1024]{3,2,1,0:T(8,128)} custom-call(f32[4,1,1,256,512]{4,3,2,1,0:T(8,128)S(1)} %copy-done, f32[256,256]{1,0:T(8,128)S(1)} %apply.12.here_ref, f32[256,256]{1,0:T(8,128)S(1)} %collective-permute-done.3.there_ref, f32[1,1,256,1024]{3,2,1,0:T(8,128)} %finish.6.refs_0_), custom_call_target="tpu_custom_call", output_to_operand_aliasing={{}: (3, {})} | custom-call | flops 201326592 | bytes 786432 | tf_op jit(solution)/shard_map/finish/pallas_call | solution.py:115
Async XLA Ops:
  0.0 1.2 %copy-start.1 = (f32[1,1,256,1024]{3,2,1,0:T(8,128)S(1)}, f32[1,1,256,1024]{3,2,1,0:T(8,128)}, u32[]{:S(2)}) copy-start(f32[1,1,256,1024]{3,2,1,0:T(8,128)} %param.2) | copy-start | bytes 3145732
  1.2 18.5 %copy-start = (f32[4,1,1,256,512]{4,3,2,1,0:T(8,128)S(1)}, f32[4,1,1,256,512]{4,3,2,1,0:T(8,128)}, u32[]{:S(2)}) copy-start(f32[4,1,1,256,512]{4,3,2,1,0:T(8,128)} %blocks_ref.27) | copy-start | bytes 6291460
  1.4 18.3 %collective-permute-start = (f32[256,512]{1,0:T(8,128)S(1)}, f32[256,512]{1,0:T(8,128)S(1)}, u32[]{:S(2)}, u32[]{:S(2)}) collective-permute-start(f32[256,512]{1,0:T(8,128)S(1)} %get-tuple-element.10.here_ref), channel_id=1, source_target_pairs={{0,256},{16,272},{32,288},{48,304},{64,320},{80,336},{96,352},{112... | collective-permute-start | bytes 1572872 | tf_op jit(solution)/shard_map/ppermute | solution.py:36
  5.5 19.8 %collective-permute-start.10 = (f32[256,256]{1,0:T(8,128)S(1)}, f32[256,256]{1,0:T(8,128)S(1)}, u32[]{:S(2)}, u32[]{:S(2)}) collective-permute-start(f32[256,256]{1,0:T(8,128)S(1)} %get-tuple-element.14.here_ref), channel_id=1, source_target_pairs={{0,256},{16,272},{32,288},{48,304},{64,320},{80,336},{96,352},{112... | collective-permute-start | bytes 786440 | tf_op jit(solution)/shard_map/ppermute | solution.py:36
  8.8 21.2 %collective-permute-start.6 = (f32[256,256]{1,0:T(8,128)S(1)}, f32[256,256]{1,0:T(8,128)S(1)}, u32[]{:S(2)}, u32[]{:S(2)}) collective-permute-start(f32[256,256]{1,0:T(8,128)S(1)} %get-tuple-element.13.here_ref), channel_id=1, source_target_pairs={{0,256},{16,272},{32,288},{48,304},{64,320},{80,336},{96,352},{112... | collective-permute-start | bytes 786440 | tf_op jit(solution)/shard_map/ppermute | solution.py:36
  20.3 29.4 %collective-permute-start.1 = (f32[256,512]{1,0:T(8,128)S(1)}, f32[256,512]{1,0:T(8,128)S(1)}, u32[]{:S(2)}, u32[]{:S(2)}) collective-permute-start(f32[256,512]{1,0:T(8,128)S(1)} %apply.10.here_ref), channel_id=1, source_target_pairs={{0,8},{1,9},{2,10},{3,11},{4,12},{5,13},{6,14},{7,15},{8,0},{9,1},... | collective-permute-start | bytes 1572872 | tf_op jit(solution)/shard_map/ppermute | solution.py:36
  25.8 17.2 %collective-permute-start.11 = (f32[256,256]{1,0:T(8,128)S(1)}, f32[256,256]{1,0:T(8,128)S(1)}, u32[]{:S(2)}, u32[]{:S(2)}) collective-permute-start(f32[256,256]{1,0:T(8,128)S(1)} %apply.17.here_ref), channel_id=1, source_target_pairs={{0,8},{1,9},{2,10},{3,11},{4,12},{5,13},{6,14},{7,15},{8,0},{9,1},... | collective-permute-start | bytes 786440 | tf_op jit(solution)/shard_map/ppermute | solution.py:36
  30.5 15.4 %collective-permute-start.7 = (f32[256,256]{1,0:T(8,128)S(1)}, f32[256,256]{1,0:T(8,128)S(1)}, u32[]{:S(2)}, u32[]{:S(2)}) collective-permute-start(f32[256,256]{1,0:T(8,128)S(1)} %apply.14.here_ref), channel_id=1, source_target_pairs={{0,8},{1,9},{2,10},{3,11},{4,12},{5,13},{6,14},{7,15},{8,0},{9,1},... | collective-permute-start | bytes 786440 | tf_op jit(solution)/shard_map/ppermute | solution.py:36
  43.4 12.9 %collective-permute-start.12 = (f32[256,256]{1,0:T(8,128)S(1)}, f32[256,256]{1,0:T(8,128)S(1)}, u32[]{:S(2)}, u32[]{:S(2)}) collective-permute-start(f32[256,256]{1,0:T(8,128)S(1)} %apply.18.here_ref), channel_id=1, source_target_pairs={{0,128},{16,144},{32,160},{48,176},{64,192},{80,208},{96,224},{112... | collective-permute-start | bytes 786440 | tf_op jit(solution)/shard_map/ppermute | solution.py:36
  46.4 18.1 %collective-permute-start.8 = (f32[256,256]{1,0:T(8,128)S(1)}, f32[256,256]{1,0:T(8,128)S(1)}, u32[]{:S(2)}, u32[]{:S(2)}) collective-permute-start(f32[256,256]{1,0:T(8,128)S(1)} %apply.15.here_ref), channel_id=1, source_target_pairs={{0,128},{16,144},{32,160},{48,176},{64,192},{80,208},{96,224},{112... | collective-permute-start | bytes 786440 | tf_op jit(solution)/shard_map/ppermute | solution.py:36
  50.4 17.9 %collective-permute-start.4 = (f32[256,256]{1,0:T(8,128)S(1)}, f32[256,256]{1,0:T(8,128)S(1)}, u32[]{:S(2)}, u32[]{:S(2)}) collective-permute-start(f32[256,256]{1,0:T(8,128)S(1)} %get-tuple-element.12.here_ref), channel_id=1, source_target_pairs={{0,128},{16,144},{32,160},{48,176},{64,192},{80,208},{96,224},{112... | collective-permute-start | bytes 786440 | tf_op jit(solution)/shard_map/ppermute | solution.py:36
  52.9 22.3 %collective-permute-start.2 = (f32[256,256]{1,0:T(8,128)S(1)}, f32[256,256]{1,0:T(8,128)S(1)}, u32[]{:S(2)}, u32[]{:S(2)}) collective-permute-start(f32[256,256]{1,0:T(8,128)S(1)} %get-tuple-element.11.here_ref), channel_id=1, source_target_pairs={{0,128},{16,144},{32,160},{48,176},{64,192},{80,208},{96,224},{112... | collective-permute-start | bytes 786440 | tf_op jit(solution)/shard_map/ppermute | solution.py:36
  56.8 22.3 %collective-permute-start.13 = (f32[256,256]{1,0:T(8,128)S(1)}, f32[256,256]{1,0:T(8,128)S(1)}, u32[]{:S(2)}, u32[]{:S(2)}) collective-permute-start(f32[256,256]{1,0:T(8,128)S(1)} %apply.19.here_ref), channel_id=1, source_target_pairs={{0,4},{1,5},{2,6},{3,7},{4,0},{5,1},{6,2},{7,3},{8,12},{9,13},{10,... | collective-permute-start | bytes 786440 | tf_op jit(solution)/shard_map/ppermute | solution.py:36
  65.0 23.6 %collective-permute-start.9 = (f32[256,256]{1,0:T(8,128)S(1)}, f32[256,256]{1,0:T(8,128)S(1)}, u32[]{:S(2)}, u32[]{:S(2)}) collective-permute-start(f32[256,256]{1,0:T(8,128)S(1)} %apply.16.here_ref), channel_id=1, source_target_pairs={{0,4},{1,5},{2,6},{3,7},{4,0},{5,1},{6,2},{7,3},{8,12},{9,13},{10,... | collective-permute-start | bytes 786440 | tf_op jit(solution)/shard_map/ppermute | solution.py:36
  68.8 33.8 %collective-permute-start.5 = (f32[256,256]{1,0:T(8,128)S(1)}, f32[256,256]{1,0:T(8,128)S(1)}, u32[]{:S(2)}, u32[]{:S(2)}) collective-permute-start(f32[256,256]{1,0:T(8,128)S(1)} %apply.13.here_ref), channel_id=1, source_target_pairs={{0,4},{1,5},{2,6},{3,7},{4,0},{5,1},{6,2},{7,3},{8,12},{9,13},{10,... | collective-permute-start | bytes 786440 | tf_op jit(solution)/shard_map/ppermute | solution.py:36
  75.6 31.5 %collective-permute-start.3 = (f32[256,256]{1,0:T(8,128)S(1)}, f32[256,256]{1,0:T(8,128)S(1)}, u32[]{:S(2)}, u32[]{:S(2)}) collective-permute-start(f32[256,256]{1,0:T(8,128)S(1)} %apply.12.here_ref), channel_id=1, source_target_pairs={{0,4},{1,5},{2,6},{3,7},{4,0},{5,1},{6,2},{7,3},{8,12},{9,13},{10,... | collective-permute-start | bytes 786440 | tf_op jit(solution)/shard_map/ppermute | solution.py:36

commit v4 on v3

--- a/solution.py
+++ b/solution.py
@@ -8,15 +8,16 @@
 from jax.sharding import PartitionSpec as P
 
 
-BEGINS = ((0, 2, 4), (0, 2, 4), (0, 2, 4, 6), (0, 2, 4, 6))
+BEGINS = ((0, 2, 4, 7), (0, 2, 4, 7), (0, 2, 4, 7), (0, 2, 4, 7))
 ORDER = (
     ("s", 0, 0), ("s", 0, 2), ("s", 0, 4), ("d", 0, 0),
-    ("s", 1, 0), ("d", 0, 2), ("s", 1, 2), ("d", 1, 0),
-    ("s", 2, 0), ("d", 0, 4), ("s", 1, 4), ("d", 1, 2),
-    ("s", 2, 2), ("d", 2, 0), ("s", 3, 0), ("d", 2, 2),
-    ("s", 3, 2), ("d", 1, 4), ("s", 2, 4), ("s", 2, 6),
-    ("d", 2, 4), ("s", 3, 4), ("d", 2, 6), ("s", 3, 6),
-    ("d", 3, 0), ("d", 3, 2), ("d", 3, 4), ("d", 3, 6),
+    ("s", 1, 0), ("s", 0, 7), ("d", 0, 2), ("s", 1, 2),
+    ("d", 1, 0), ("s", 2, 0), ("d", 0, 4), ("s", 1, 4),
+    ("d", 1, 2), ("s", 2, 2), ("d", 2, 0), ("s", 3, 0),
+    ("d", 1, 4), ("s", 2, 4), ("d", 2, 2), ("s", 3, 2),
+    ("d", 0, 7), ("s", 1, 7), ("d", 2, 4), ("s", 3, 4),
+    ("d", 3, 0), ("d", 1, 7), ("s", 2, 7), ("d", 2, 7),
+    ("s", 3, 7), ("d", 3, 2), ("d", 3, 4), ("d", 3, 7),
 )
 LAST = 3
 EARLY = ()

time: 109 us -> 112 us (1.028)
  the two profiles are of different devices: /device:TPU:2 before, /device:TPU:128 now
where the time goes in v4:
time: 112 us; the launch traced here: 111 us
  starting transfers between devices  66.9 us (60%)
  waiting for transfers between devices  32.1 us (29%)
  Pallas kernels  10.7 us (10%)
  local copies, waits for them, and re-layouts  1.23 us (1%)
    ppermute x16, starting transfers between devices, exchange(): return lax.ppermute(block, axis, route)  66.9 us
    ppermute x16, waiting for transfers between devices, exchange(): return lax.ppermute(block, axis, route)  32.1 us
    pallas_call x12, Pallas kernels, apply(): call(kernel, out_shape=[jax.ShapeDtypeStruct((rank, b - a), here.dtype) f...  5.85 us
    pallas_call x4, Pallas kernels, apply_in_place(): call(kernel, out_shape=jax.ShapeDtypeStruct(shape, here.dtype), in_specs=...  4.75 us
  transfers between devices with their start and end apart: 16, of which 7 were waited for; matrix products, arithmetic and copies ran while one was open for 0% of the time, Pallas kernels for 8%

profile of v4, /device:TPU:128, one launch (start us, length us, event | category | flops | bytes accessed | tf_op | source)
XLA Modules:
  0.0 111.2 jit_solution(12811747954843119767)
XLA Ops:
  0.0 1.2 %copy-done.1 = f32[1,1,256,1024]{3,2,1,0:T(8,128)S(1)} copy-done((f32[1,1,256,1024]{3,2,1,0:T(8,128)S(1)}, f32[1,1,256,1024]{3,2,1,0:T(8,128)}, u32[]{:S(2)}) %copy-start.1) | copy-done | bytes 1048600
  1.2 0.1 split.1
  1.4 5.1 %collective-permute-start.4 = (f32[256,384]{1,0:T(8,128)S(1)}, f32[256,384]{1,0:T(8,128)S(1)}, u32[]{:S(2)}, u32[]{:S(2)}) collective-permute-start(f32[256,384]{1,0:T(8,128)S(1)} %get-tuple-element.10.here_ref), channel_id=1, source_target_pairs={{0,256},{16,272},{32,288},{48,304},{64,320},{80,336},{96,352},{112... | collective-permute-start | bytes 1179656 | tf_op jit(solution)/shard_map/ppermute | solution.py:37
  6.4 9.3 %collective-permute-done.4.there_ref = f32[256,384]{1,0:T(8,128)S(1)} collective-permute-done((f32[256,384]{1,0:T(8,128)S(1)}, f32[256,384]{1,0:T(8,128)S(1)}, u32[]{:S(2)}, u32[]{:S(2)}) %collective-permute-start.4) | collective-permute-done | bytes 393248 | tf_op jit(solution)/shard_map/ppermute | solution.py:37
  15.8 0.6 apply.15.here_ref
  16.4 4.3 %collective-permute-start.5 = (f32[256,384]{1,0:T(8,128)S(1)}, f32[256,384]{1,0:T(8,128)S(1)}, u32[]{:S(2)}, u32[]{:S(2)}) collective-permute-start(f32[256,384]{1,0:T(8,128)S(1)} %apply.15.here_ref), channel_id=1, source_target_pairs={{0,8},{1,9},{2,10},{3,11},{4,12},{5,13},{6,14},{7,15},{8,0},{9,1},... | collective-permute-start | bytes 1179656 | tf_op jit(solution)/shard_map/ppermute | solution.py:37
  20.7 4.9 %collective-permute-start.12 = (f32[256,256]{1,0:T(8,128)S(1)}, f32[256,256]{1,0:T(8,128)S(1)}, u32[]{:S(2)}, u32[]{:S(2)}) collective-permute-start(f32[256,256]{1,0:T(8,128)S(1)} %get-tuple-element.12.here_ref), channel_id=1, source_target_pairs={{0,256},{16,272},{32,288},{48,304},{64,320},{80,336},{96,352},{112... | collective-permute-start | bytes 786440 | tf_op jit(solution)/shard_map/ppermute | solution.py:37
  25.6 2.4 %collective-permute-start.8 = (f32[256,256]{1,0:T(8,128)S(1)}, f32[256,256]{1,0:T(8,128)S(1)}, u32[]{:S(2)}, u32[]{:S(2)}) collective-permute-start(f32[256,256]{1,0:T(8,128)S(1)} %get-tuple-element.11.here_ref), channel_id=1, source_target_pairs={{0,256},{16,272},{32,288},{48,304},{64,320},{80,336},{96,352},{112... | collective-permute-start | bytes 786440 | tf_op jit(solution)/shard_map/ppermute | solution.py:37
  28.1 4.2 %collective-permute-done.12.there_ref = f32[256,256]{1,0:T(8,128)S(1)} collective-permute-done((f32[256,256]{1,0:T(8,128)S(1)}, f32[256,256]{1,0:T(8,128)S(1)}, u32[]{:S(2)}, u32[]{:S(2)}) %collective-permute-start.12) | collective-permute-done | bytes 262176 | tf_op jit(solution)/shard_map/ppermute | solution.py:37
  32.3 0.4 apply.21.here_ref
  32.8 1.9 %collective-permute-start.13 = (f32[256,256]{1,0:T(8,128)S(1)}, f32[256,256]{1,0:T(8,128)S(1)}, u32[]{:S(2)}, u32[]{:S(2)}) collective-permute-start(f32[256,256]{1,0:T(8,128)S(1)} %apply.21.here_ref), channel_id=1, source_target_pairs={{0,8},{1,9},{2,10},{3,11},{4,12},{5,13},{6,14},{7,15},{8,0},{9,1},... | collective-permute-start | bytes 786440 | tf_op jit(solution)/shard_map/ppermute | solution.py:37
  34.7 1.9 %collective-permute-done.8.there_ref = f32[256,256]{1,0:T(8,128)S(1)} collective-permute-done((f32[256,256]{1,0:T(8,128)S(1)}, f32[256,256]{1,0:T(8,128)S(1)}, u32[]{:S(2)}, u32[]{:S(2)}) %collective-permute-start.8) | collective-permute-done | bytes 262176 | tf_op jit(solution)/shard_map/ppermute | solution.py:37
  36.6 0.4 apply.18.here_ref
  37.1 2.2 %collective-permute-start.9 = (f32[256,256]{1,0:T(8,128)S(1)}, f32[256,256]{1,0:T(8,128)S(1)}, u32[]{:S(2)}, u32[]{:S(2)}) collective-permute-start(f32[256,256]{1,0:T(8,128)S(1)} %apply.18.here_ref), channel_id=1, source_target_pairs={{0,8},{1,9},{2,10},{3,11},{4,12},{5,13},{6,14},{7,15},{8,0},{9,1},... | collective-permute-start | bytes 786440 | tf_op jit(solution)/shard_map/ppermute | solution.py:37
  39.3 0.0 collective-permute-done.5.there_ref
  39.3 0.6 apply.16.here_ref
  39.9 3.8 %collective-permute-start.6 = (f32[256,384]{1,0:T(8,128)S(1)}, f32[256,384]{1,0:T(8,128)S(1)}, u32[]{:S(2)}, u32[]{:S(2)}) collective-permute-start(f32[256,384]{1,0:T(8,128)S(1)} %apply.16.here_ref), channel_id=1, source_target_pairs={{0,128},{16,144},{32,160},{48,176},{64,192},{80,208},{96,224},{112... | collective-permute-start | bytes 1179656 | tf_op jit(solution)/shard_map/ppermute | solution.py:37
  43.7 0.0 collective-permute-done.13.there_ref
  43.7 0.5 apply.22.here_ref
  44.2 3.0 %collective-permute-start.14 = (f32[256,256]{1,0:T(8,128)S(1)}, f32[256,256]{1,0:T(8,128)S(1)}, u32[]{:S(2)}, u32[]{:S(2)}) collective-permute-start(f32[256,256]{1,0:T(8,128)S(1)} %apply.22.here_ref), channel_id=1, source_target_pairs={{0,128},{16,144},{32,160},{48,176},{64,192},{80,208},{96,224},{112... | collective-permute-start | bytes 786440 | tf_op jit(solution)/shard_map/ppermute | solution.py:37
  47.2 0.0 collective-permute-done.9.there_ref
  47.2 0.4 apply.19.here_ref
  47.7 3.4 %collective-permute-start.10 = (f32[256,256]{1,0:T(8,128)S(1)}, f32[256,256]{1,0:T(8,128)S(1)}, u32[]{:S(2)}, u32[]{:S(2)}) collective-permute-start(f32[256,256]{1,0:T(8,128)S(1)} %apply.19.here_ref), channel_id=1, source_target_pairs={{0,128},{16,144},{32,160},{48,176},{64,192},{80,208},{96,224},{112... | collective-permute-start | bytes 786440 | tf_op jit(solution)/shard_map/ppermute | solution.py:37
  51.1 5.2 %collective-permute-start = (f32[256,128]{1,0:T(8,128)S(1)}, f32[256,128]{1,0:T(8,128)S(1)}, u32[]{:S(2)}, u32[]{:S(2)}) collective-permute-start(f32[256,128]{1,0:T(8,128)S(1)} %get-tuple-element.9.here_ref), channel_id=1, source_target_pairs={{0,256},{16,272},{32,288},{48,304},{64,320},{80,336},{96,352},{112... | collective-permute-start | bytes 393224 | tf_op jit(solution)/shard_map/ppermute | solution.py:37
  56.3 0.0 collective-permute-done.6.there_ref
  56.3 0.6 apply.17.here_ref
  56.9 7.7 %collective-permute-start.7 = (f32[256,384]{1,0:T(8,128)S(1)}, f32[256,384]{1,0:T(8,128)S(1)}, u32[]{:S(2)}, u32[]{:S(2)}) collective-permute-start(f32[256,384]{1,0:T(8,128)S(1)} %apply.17.here_ref), channel_id=1, source_target_pairs={{0,4},{1,5},{2,6},{3,7},{4,0},{5,1},{6,2},{7,3},{8,12},{9,13},{10,... | collective-permute-start | bytes 1179656 | tf_op jit(solution)/shard_map/ppermute | solution.py:37
  64.7 2.2 %collective-permute-done.there_ref = f32[256,128]{1,0:T(8,128)S(1)} collective-permute-done((f32[256,128]{1,0:T(8,128)S(1)}, f32[256,128]{1,0:T(8,128)S(1)}, u32[]{:S(2)}, u32[]{:S(2)}) %collective-permute-start) | collective-permute-done | bytes 131104 | tf_op jit(solution)/shard_map/ppermute | solution.py:37
  66.9 0.4 apply.12.here_ref
  67.3 3.4 %collective-permute-start.1 = (f32[256,128]{1,0:T(8,128)S(1)}, f32[256,128]{1,0:T(8,128)S(1)}, u32[]{:S(2)}, u32[]{:S(2)}) collective-permute-start(f32[256,128]{1,0:T(8,128)S(1)} %apply.12.here_ref), channel_id=1, source_target_pairs={{0,8},{1,9},{2,10},{3,11},{4,12},{5,13},{6,14},{7,15},{8,0},{9,1},... | collective-permute-start | bytes 393224 | tf_op jit(solution)/shard_map/ppermute | solution.py:37
  70.7 0.0 collective-permute-done.14.there_ref
  70.7 0.5 apply.23.here_ref
  71.2 7.7 %collective-permute-start.15 = (f32[256,256]{1,0:T(8,128)S(1)}, f32[256,256]{1,0:T(8,128)S(1)}, u32[]{:S(2)}, u32[]{:S(2)}) collective-permute-start(f32[256,256]{1,0:T(8,128)S(1)} %apply.23.here_ref), channel_id=1, source_target_pairs={{0,4},{1,5},{2,6},{3,7},{4,0},{5,1},{6,2},{7,3},{8,12},{9,13},{10,... | collective-permute-start | bytes 786440 | tf_op jit(solution)/shard_map/ppermute | solution.py:37
  78.9 0.4 apply.20.here_ref
  79.4 2.0 %collective-permute-start.11 = (f32[256,256]{1,0:T(8,128)S(1)}, f32[256,256]{1,0:T(8,128)S(1)}, u32[]{:S(2)}, u32[]{:S(2)}) collective-permute-start(f32[256,256]{1,0:T(8,128)S(1)} %apply.20.here_ref), channel_id=1, source_target_pairs={{0,4},{1,5},{2,6},{3,7},{4,0},{5,1},{6,2},{7,3},{8,12},{9,13},{10,... | collective-permute-start | bytes 786440 | tf_op jit(solution)/shard_map/ppermute | solution.py:37
  81.4 0.4 apply.13.here_ref
  81.9 2.1 %collective-permute-start.2 = (f32[256,128]{1,0:T(8,128)S(1)}, f32[256,128]{1,0:T(8,128)S(1)}, u32[]{:S(2)}, u32[]{:S(2)}) collective-permute-start(f32[256,128]{1,0:T(8,128)S(1)} %apply.13.here_ref), channel_id=1, source_target_pairs={{0,128},{16,144},{32,160},{48,176},{64,192},{80,208},{96,224},{112... | collective-permute-start | bytes 393224 | tf_op jit(solution)/shard_map/ppermute | solution.py:37
  84.0 4.7 %collective-permute-done.2.there_ref = f32[256,128]{1,0:T(8,128)S(1)} collective-permute-done((f32[256,128]{1,0:T(8,128)S(1)}, f32[256,128]{1,0:T(8,128)S(1)}, u32[]{:S(2)}, u32[]{:S(2)}) %collective-permute-start.2) | collective-permute-done | bytes 131104 | tf_op jit(solution)/shard_map/ppermute | solution.py:37
  88.7 0.4 apply.14.here_ref
  89.1 7.7 %collective-permute-start.3 = (f32[256,128]{1,0:T(8,128)S(1)}, f32[256,128]{1,0:T(8,128)S(1)}, u32[]{:S(2)}, u32[]{:S(2)}) collective-permute-start(f32[256,128]{1,0:T(8,128)S(1)} %apply.14.here_ref), channel_id=1, source_target_pairs={{0,4},{1,5},{2,6},{3,7},{4,0},{5,1},{6,2},{7,3},{8,12},{9,13},{10,... | collective-permute-start | bytes 393224 | tf_op jit(solution)/shard_map/ppermute | solution.py:37
  96.9 1.9 %collective-permute-done.15.there_ref = f32[256,256]{1,0:T(8,128)S(1)} collective-permute-done((f32[256,256]{1,0:T(8,128)S(1)}, f32[256,256]{1,0:T(8,128)S(1)}, u32[]{:S(2)}, u32[]{:S(2)}) %collective-permute-start.15) | collective-permute-done | bytes 262176 | tf_op jit(solution)/shard_map/ppermute | solution.py:37
  98.8 1.2 %finish.4.refs_0_ = f32[1,1,256,1024]{3,2,1,0:T(8,128)} custom-call(f32[4,1,1,256,512]{4,3,2,1,0:T(8,128)S(1)} %copy-done, f32[256,256]{1,0:T(8,128)S(1)} %apply.23.here_ref, f32[256,256]{1,0:T(8,128)S(1)} %collective-permute-done.15.there_ref), custom_call_target="tpu_custom_call" | custom-call | flops 201326592 | bytes 786432 | tf_op jit(solution)/shard_map/finish/pallas_call | solution.py:116
  99.9 7.7 %collective-permute-done.11.there_ref = f32[256,256]{1,0:T(8,128)S(1)} collective-permute-done((f32[256,256]{1,0:T(8,128)S(1)}, f32[256,256]{1,0:T(8,128)S(1)}, u32[]{:S(2)}, u32[]{:S(2)}) %collective-permute-start.11) | collective-permute-done | bytes 262176 | tf_op jit(solution)/shard_map/ppermute | solution.py:37
  107.6 1.1 %finish.5.refs_0_ = f32[1,1,256,1024]{3,2,1,0:T(8,128)} custom-call(f32[4,1,1,256,512]{4,3,2,1,0:T(8,128)S(1)} %copy-done, f32[256,256]{1,0:T(8,128)S(1)} %apply.20.here_ref, f32[256,256]{1,0:T(8,128)S(1)} %collective-permute-done.11.there_ref, f32[1,1,256,1024]{3,2,1,0:T(8,128)} %finish.4.refs_0_), custom_call_target="tpu_custom_call", output_to_operand_aliasing={{}: (3, {})} | custom-call | flops 201326592 | bytes 786432 | tf_op jit(solution)/shard_map/finish/pallas_call | solution.py:116
  108.7 0.0 collective-permute-done.7.there_ref
  108.7 1.4 %finish.6.refs_0_ = f32[1,1,256,1024]{3,2,1,0:T(8,128)} custom-call(f32[4,1,1,256,512]{4,3,2,1,0:T(8,128)S(1)} %copy-done, f32[256,384]{1,0:T(8,128)S(1)} %apply.17.here_ref, f32[256,384]{1,0:T(8,128)S(1)} %collective-permute-done.7.there_ref, f32[1,1,256,1024]{3,2,1,0:T(8,128)} %finish.5.refs_0_), custom_call_target="tpu_custom_call", output_to_operand_aliasing={{}: (3, {})} | custom-call | flops 301989888 | bytes 1179648 | tf_op jit(solution)/shard_map/finish/pallas_call | solution.py:116
  110.1 0.0 collective-permute-done.3.there_ref
  110.1 1.1 finish.7
  (5 shorter events, 0.0 us)
Async XLA Ops:
  0.0 1.2 %copy-start.1 = (f32[1,1,256,1024]{3,2,1,0:T(8,128)S(1)}, f32[1,1,256,1024]{3,2,1,0:T(8,128)}, u32[]{:S(2)}) copy-start(f32[1,1,256,1024]{3,2,1,0:T(8,128)} %param.2) | copy-start | bytes 3145732
  1.2 14.5 %copy-start = (f32[4,1,1,256,512]{4,3,2,1,0:T(8,128)S(1)}, f32[4,1,1,256,512]{4,3,2,1,0:T(8,128)}, u32[]{:S(2)}) copy-start(f32[4,1,1,256,512]{4,3,2,1,0:T(8,128)} %blocks_ref.31) | copy-start | bytes 6291460
  1.4 14.4 %collective-permute-start.4 = (f32[256,384]{1,0:T(8,128)S(1)}, f32[256,384]{1,0:T(8,128)S(1)}, u32[]{:S(2)}, u32[]{:S(2)}) collective-permute-start(f32[256,384]{1,0:T(8,128)S(1)} %get-tuple-element.10.here_ref), channel_id=1, source_target_pairs={{0,256},{16,272},{32,288},{48,304},{64,320},{80,336},{96,352},{112... | collective-permute-start | bytes 1179656 | tf_op jit(solution)/shard_map/ppermute | solution.py:37
  16.4 22.9 %collective-permute-start.5 = (f32[256,384]{1,0:T(8,128)S(1)}, f32[256,384]{1,0:T(8,128)S(1)}, u32[]{:S(2)}, u32[]{:S(2)}) collective-permute-start(f32[256,384]{1,0:T(8,128)S(1)} %apply.15.here_ref), channel_id=1, source_target_pairs={{0,8},{1,9},{2,10},{3,11},{4,12},{5,13},{6,14},{7,15},{8,0},{9,1},... | collective-permute-start | bytes 1179656 | tf_op jit(solution)/shard_map/ppermute | solution.py:37
  20.7 11.6 %collective-permute-start.12 = (f32[256,256]{1,0:T(8,128)S(1)}, f32[256,256]{1,0:T(8,128)S(1)}, u32[]{:S(2)}, u32[]{:S(2)}) collective-permute-start(f32[256,256]{1,0:T(8,128)S(1)} %get-tuple-element.12.here_ref), channel_id=1, source_target_pairs={{0,256},{16,272},{32,288},{48,304},{64,320},{80,336},{96,352},{112... | collective-permute-start | bytes 786440 | tf_op jit(solution)/shard_map/ppermute | solution.py:37
  25.6 11.0 %collective-permute-start.8 = (f32[256,256]{1,0:T(8,128)S(1)}, f32[256,256]{1,0:T(8,128)S(1)}, u32[]{:S(2)}, u32[]{:S(2)}) collective-permute-start(f32[256,256]{1,0:T(8,128)S(1)} %get-tuple-element.11.here_ref), channel_id=1, source_target_pairs={{0,256},{16,272},{32,288},{48,304},{64,320},{80,336},{96,352},{112... | collective-permute-start | bytes 786440 | tf_op jit(solution)/shard_map/ppermute | solution.py:37
  32.8 10.9 %collective-permute-start.13 = (f32[256,256]{1,0:T(8,128)S(1)}, f32[256,256]{1,0:T(8,128)S(1)}, u32[]{:S(2)}, u32[]{:S(2)}) collective-permute-start(f32[256,256]{1,0:T(8,128)S(1)} %apply.21.here_ref), channel_id=1, source_target_pairs={{0,8},{1,9},{2,10},{3,11},{4,12},{5,13},{6,14},{7,15},{8,0},{9,1},... | collective-permute-start | bytes 786440 | tf_op jit(solution)/shard_map/ppermute | solution.py:37
  37.1 10.1 %collective-permute-start.9 = (f32[256,256]{1,0:T(8,128)S(1)}, f32[256,256]{1,0:T(8,128)S(1)}, u32[]{:S(2)}, u32[]{:S(2)}) collective-permute-start(f32[256,256]{1,0:T(8,128)S(1)} %apply.18.here_ref), channel_id=1, source_target_pairs={{0,8},{1,9},{2,10},{3,11},{4,12},{5,13},{6,14},{7,15},{8,0},{9,1},... | collective-permute-start | bytes 786440 | tf_op jit(solution)/shard_map/ppermute | solution.py:37
  39.9 16.3 %collective-permute-start.6 = (f32[256,384]{1,0:T(8,128)S(1)}, f32[256,384]{1,0:T(8,128)S(1)}, u32[]{:S(2)}, u32[]{:S(2)}) collective-permute-start(f32[256,384]{1,0:T(8,128)S(1)} %apply.16.here_ref), channel_id=1, source_target_pairs={{0,128},{16,144},{32,160},{48,176},{64,192},{80,208},{96,224},{112... | collective-permute-start | bytes 1179656 | tf_op jit(solution)/shard_map/ppermute | solution.py:37
  44.2 26.5 %collective-permute-start.14 = (f32[256,256]{1,0:T(8,128)S(1)}, f32[256,256]{1,0:T(8,128)S(1)}, u32[]{:S(2)}, u32[]{:S(2)}) collective-permute-start(f32[256,256]{1,0:T(8,128)S(1)} %apply.22.here_ref), channel_id=1, source_target_pairs={{0,128},{16,144},{32,160},{48,176},{64,192},{80,208},{96,224},{112... | collective-permute-start | bytes 786440 | tf_op jit(solution)/shard_map/ppermute | solution.py:37
  47.7 31.2 %collective-permute-start.10 = (f32[256,256]{1,0:T(8,128)S(1)}, f32[256,256]{1,0:T(8,128)S(1)}, u32[]{:S(2)}, u32[]{:S(2)}) collective-permute-start(f32[256,256]{1,0:T(8,128)S(1)} %apply.19.here_ref), channel_id=1, source_target_pairs={{0,128},{16,144},{32,160},{48,176},{64,192},{80,208},{96,224},{112... | collective-permute-start | bytes 786440 | tf_op jit(solution)/shard_map/ppermute | solution.py:37
  51.1 15.9 %collective-permute-start = (f32[256,128]{1,0:T(8,128)S(1)}, f32[256,128]{1,0:T(8,128)S(1)}, u32[]{:S(2)}, u32[]{:S(2)}) collective-permute-start(f32[256,128]{1,0:T(8,128)S(1)} %get-tuple-element.9.here_ref), channel_id=1, source_target_pairs={{0,256},{16,272},{32,288},{48,304},{64,320},{80,336},{96,352},{112... | collective-permute-start | bytes 393224 | tf_op jit(solution)/shard_map/ppermute | solution.py:37
  56.9 51.8 %collective-permute-start.7 = (f32[256,384]{1,0:T(8,128)S(1)}, f32[256,384]{1,0:T(8,128)S(1)}, u32[]{:S(2)}, u32[]{:S(2)}) collective-permute-start(f32[256,384]{1,0:T(8,128)S(1)} %apply.17.here_ref), channel_id=1, source_target_pairs={{0,4},{1,5},{2,6},{3,7},{4,0},{5,1},{6,2},{7,3},{8,12},{9,13},{10,... | collective-permute-start | bytes 1179656 | tf_op jit(solution)/shard_map/ppermute | solution.py:37
  67.3 14.1 %collective-permute-start.1 = (f32[256,128]{1,0:T(8,128)S(1)}, f32[256,128]{1,0:T(8,128)S(1)}, u32[]{:S(2)}, u32[]{:S(2)}) collective-permute-start(f32[256,128]{1,0:T(8,128)S(1)} %apply.12.here_ref), channel_id=1, source_target_pairs={{0,8},{1,9},{2,10},{3,11},{4,12},{5,13},{6,14},{7,15},{8,0},{9,1},... | collective-permute-start | bytes 393224 | tf_op jit(solution)/shard_map/ppermute | solution.py:37
  71.2 27.6 %collective-permute-start.15 = (f32[256,256]{1,0:T(8,128)S(1)}, f32[256,256]{1,0:T(8,128)S(1)}, u32[]{:S(2)}, u32[]{:S(2)}) collective-permute-start(f32[256,256]{1,0:T(8,128)S(1)} %apply.23.here_ref), channel_id=1, source_target_pairs={{0,4},{1,5},{2,6},{3,7},{4,0},{5,1},{6,2},{7,3},{8,12},{9,13},{10,... | collective-permute-start | bytes 786440 | tf_op jit(solution)/shard_map/ppermute | solution.py:37
  79.4 28.2 %collective-permute-start.11 = (f32[256,256]{1,0:T(8,128)S(1)}, f32[256,256]{1,0:T(8,128)S(1)}, u32[]{:S(2)}, u32[]{:S(2)}) collective-permute-start(f32[256,256]{1,0:T(8,128)S(1)} %apply.20.here_ref), channel_id=1, source_target_pairs={{0,4},{1,5},{2,6},{3,7},{4,0},{5,1},{6,2},{7,3},{8,12},{9,13},{10,... | collective-permute-start | bytes 786440 | tf_op jit(solution)/shard_map/ppermute | solution.py:37
  81.9 6.9 %collective-permute-start.2 = (f32[256,128]{1,0:T(8,128)S(1)}, f32[256,128]{1,0:T(8,128)S(1)}, u32[]{:S(2)}, u32[]{:S(2)}) collective-permute-start(f32[256,128]{1,0:T(8,128)S(1)} %apply.13.here_ref), channel_id=1, source_target_pairs={{0,128},{16,144},{32,160},{48,176},{64,192},{80,208},{96,224},{112... | collective-permute-start | bytes 393224 | tf_op jit(solution)/shard_map/ppermute | solution.py:37
  89.1 21.0 %collective-permute-start.3 = (f32[256,128]{1,0:T(8,128)S(1)}, f32[256,128]{1,0:T(8,128)S(1)}, u32[]{:S(2)}, u32[]{:S(2)}) collective-permute-start(f32[256,128]{1,0:T(8,128)S(1)} %apply.14.here_ref), channel_id=1, source_target_pairs={{0,4},{1,5},{2,6},{3,7},{4,0},{5,1},{6,2},{7,3},{8,12},{9,13},{10,... | collective-permute-start | bytes 393224 | tf_op jit(solution)/shard_map/ppermute | solution.py:37

commit v5 on v4

--- a/solution.py
+++ b/solution.py
@@ -12,8 +12,8 @@
 ORDER = (
     ("s", 0, 0), ("s", 0, 2), ("s", 0, 4), ("d", 0, 0),
     ("s", 1, 0), ("s", 0, 7), ("d", 0, 2), ("s", 1, 2),
-    ("d", 1, 0), ("s", 2, 0), ("d", 0, 4), ("s", 1, 4),
-    ("d", 1, 2), ("s", 2, 2), ("d", 2, 0), ("s", 3, 0),
+    ("d", 1, 0), ("s", 2, 0), ("d", 1, 2), ("s", 2, 2),
+    ("d", 0, 4), ("s", 1, 4), ("d", 2, 0), ("s", 3, 0),
     ("d", 1, 4), ("s", 2, 4), ("d", 2, 2), ("s", 3, 2),
     ("d", 0, 7), ("s", 1, 7), ("d", 2, 4), ("s", 3, 4),
     ("d", 3, 0), ("d", 1, 7), ("s", 2, 7), ("d", 2, 7),
@@ -65,36 +65,23 @@
     axis, bit = plan()[level]
     rank = here.shape[0]
     upper = jnp.bitwise_and(jnp.right_shift(lax.axis_index(axis), bit), 1)
-    mine = blocks_ref[:, pl.ds(pl.multiple_of(upper * rank, rank), rank)]
-    other = blocks_ref[:, pl.ds(pl.multiple_of((1 - upper) * rank, rank), rank)]
+    mine = blocks_ref[level, 0, 0, :, pl.ds(pl.multiple_of(upper * rank, rank), rank)]
+    other = blocks_ref[level, 0, 0, :, pl.ds(pl.multiple_of((1 - upper) * rank, rank), rank)]
     return dot(mine, here) + dot(other, there)
-
-
-def fetch(level, blocks_ref, held_ref, sem):
-    copy = pltpu.make_async_copy(blocks_ref.at[level, 0, 0], held_ref, sem)
-    copy.start()
-    copy.wait()
-
-
-def held(blocks):
-    return [pltpu.VMEM(blocks.shape[3:], blocks.dtype), pltpu.SemaphoreType.DMA]
 
 
 def apply(level, blocks, here, there, spans, limit):
     rank = here.shape[0]
 
     def kernel(blocks_ref, here_ref, there_ref, *refs):
-        *outs, held_ref, sem = refs
-        fetch(level, blocks_ref, held_ref, sem)
-        for (a, b), out in zip(spans, outs):
-            out[...] = products(level, held_ref, here_ref[:, a:b], there_ref[:, a:b])
+        for (a, b), out in zip(spans, refs):
+            out[...] = products(level, blocks_ref, here_ref[:, a:b], there_ref[:, a:b])
 
     return call(
         kernel,
         out_shape=[jax.ShapeDtypeStruct((rank, b - a), here.dtype) for a, b in spans],
-        in_specs=[ANY, VMEM, VMEM],
+        in_specs=[VMEM, VMEM, VMEM],
         out_specs=[VMEM] * len(spans),
-        scratch_shapes=held(blocks),
         cost_estimate=cost(here.shape),
         limit=limit,
         name="apply",
@@ -105,9 +92,8 @@
     a, b = span
 
     def kernel(blocks_ref, here_ref, there_ref, *refs):
-        out_ref, sum_ref, held_ref, sem = refs[-4:]
-        fetch(level, blocks_ref, held_ref, sem)
-        sum_ref[...] = products(level, held_ref, here_ref[...], there_ref[...])
+        out_ref, sum_ref, sem = refs[-3:]
+        sum_ref[...] = products(level, blocks_ref, here_ref[...], there_ref[...])
         copy = pltpu.make_async_copy(sum_ref, out_ref.at[0, 0, :, a:b], sem)
         copy.start()
         copy.wait()
@@ -116,10 +102,10 @@
     return call(
         kernel,
         out_shape=jax.ShapeDtypeStruct(shape, here.dtype),
-        in_specs=[ANY, VMEM, VMEM, ANY][: len(operands)],
+        in_specs=[VMEM, VMEM, VMEM, ANY][: len(operands)],
         out_specs=ANY,
         input_output_aliases={} if whole is None else {3: 0},
-        scratch_shapes=[pltpu.VMEM(here.shape, here.dtype)] + held(blocks),
+        scratch_shapes=[pltpu.VMEM(here.shape, here.dtype), pltpu.SemaphoreType.DMA],
         cost_estimate=cost(here.shape),
         name="finish",
     )(*operands)

time: 112 us -> 111 us (level)
  transfers between devices with their start and end apart: 16 -> 16, of which waited for: 7 -> 7; matrix products, arithmetic and copies ran while one was open for 0% -> 0% of each run, Pallas kernels for 8% -> 7%
where the time goes in v5:
time: 111 us
  starting transfers between devices  67 us (60%)
  waiting for transfers between devices  32.4 us (29%)
  Pallas kernels  9.93 us (9%)
  local copies, waits for them, and re-layouts  1.23 us (1%)
    ppermute x16, starting transfers between devices, exchange(): return lax.ppermute(block, axis, route)  67 us
    ppermute x16, waiting for transfers between devices, exchange(): return lax.ppermute(block, axis, route)  32.4 us
    pallas_call x12, Pallas kernels, apply(): call(kernel, out_shape=[jax.ShapeDtypeStruct((rank, b - a), here.dtype) f...  5.21 us
    pallas_call x4, Pallas kernels, apply_in_place(): call(kernel, out_shape=jax.ShapeDtypeStruct(shape, here.dtype), in_specs=...  4.59 us
  transfers between devices with their start and end apart: 16, of which 7 were waited for; matrix products, arithmetic and copies ran while one was open for 0% of the time, Pallas kernels for 7%

profile of v5, /device:TPU:128, one launch (start us, length us, event | category | flops | bytes accessed | tf_op | source)
XLA Modules:
  0.0 110.8 jit_solution(16944592873090715554)
XLA Ops:
  0.0 1.2 %copy-done.1 = f32[1,1,256,1024]{3,2,1,0:T(8,128)S(1)} copy-done((f32[1,1,256,1024]{3,2,1,0:T(8,128)S(1)}, f32[1,1,256,1024]{3,2,1,0:T(8,128)}, u32[]{:S(2)}) %copy-start.1) | copy-done | bytes 1048600
  1.2 0.1 split.1
  1.4 5.1 %collective-permute-start.4 = (f32[256,384]{1,0:T(8,128)S(1)}, f32[256,384]{1,0:T(8,128)S(1)}, u32[]{:S(2)}, u32[]{:S(2)}) collective-permute-start(f32[256,384]{1,0:T(8,128)S(1)} %get-tuple-element.10.here_ref), channel_id=1, source_target_pairs={{0,256},{16,272},{32,288},{48,304},{64,320},{80,336},{96,352},{112... | collective-permute-start | bytes 1179656 | tf_op jit(solution)/shard_map/ppermute | solution.py:37
  6.4 9.3 %collective-permute-done.4.there_ref = f32[256,384]{1,0:T(8,128)S(1)} collective-permute-done((f32[256,384]{1,0:T(8,128)S(1)}, f32[256,384]{1,0:T(8,128)S(1)}, u32[]{:S(2)}, u32[]{:S(2)}) %collective-permute-start.4) | collective-permute-done | bytes 393248 | tf_op jit(solution)/shard_map/ppermute | solution.py:37
  15.8 0.6 apply.15.here_ref
  16.3 4.3 %collective-permute-start.5 = (f32[256,384]{1,0:T(8,128)S(1)}, f32[256,384]{1,0:T(8,128)S(1)}, u32[]{:S(2)}, u32[]{:S(2)}) collective-permute-start(f32[256,384]{1,0:T(8,128)S(1)} %apply.15.here_ref), channel_id=1, source_target_pairs={{0,8},{1,9},{2,10},{3,11},{4,12},{5,13},{6,14},{7,15},{8,0},{9,1},... | collective-permute-start | bytes 1179656 | tf_op jit(solution)/shard_map/ppermute | solution.py:37
  20.6 4.9 %collective-permute-start.12 = (f32[256,256]{1,0:T(8,128)S(1)}, f32[256,256]{1,0:T(8,128)S(1)}, u32[]{:S(2)}, u32[]{:S(2)}) collective-permute-start(f32[256,256]{1,0:T(8,128)S(1)} %get-tuple-element.12.here_ref), channel_id=1, source_target_pairs={{0,256},{16,272},{32,288},{48,304},{64,320},{80,336},{96,352},{112... | collective-permute-start | bytes 786440 | tf_op jit(solution)/shard_map/ppermute | solution.py:37
  25.6 2.4 %collective-permute-start.8 = (f32[256,256]{1,0:T(8,128)S(1)}, f32[256,256]{1,0:T(8,128)S(1)}, u32[]{:S(2)}, u32[]{:S(2)}) collective-permute-start(f32[256,256]{1,0:T(8,128)S(1)} %get-tuple-element.11.here_ref), channel_id=1, source_target_pairs={{0,256},{16,272},{32,288},{48,304},{64,320},{80,336},{96,352},{112... | collective-permute-start | bytes 786440 | tf_op jit(solution)/shard_map/ppermute | solution.py:37
  28.0 4.2 %collective-permute-done.12.there_ref = f32[256,256]{1,0:T(8,128)S(1)} collective-permute-done((f32[256,256]{1,0:T(8,128)S(1)}, f32[256,256]{1,0:T(8,128)S(1)}, u32[]{:S(2)}, u32[]{:S(2)}) %collective-permute-start.12) | collective-permute-done | bytes 262176 | tf_op jit(solution)/shard_map/ppermute | solution.py:37
  32.2 0.4 apply.21.here_ref
  32.6 1.9 %collective-permute-start.13 = (f32[256,256]{1,0:T(8,128)S(1)}, f32[256,256]{1,0:T(8,128)S(1)}, u32[]{:S(2)}, u32[]{:S(2)}) collective-permute-start(f32[256,256]{1,0:T(8,128)S(1)} %apply.21.here_ref), channel_id=1, source_target_pairs={{0,8},{1,9},{2,10},{3,11},{4,12},{5,13},{6,14},{7,15},{8,0},{9,1},... | collective-permute-start | bytes 786440 | tf_op jit(solution)/shard_map/ppermute | solution.py:37
  34.6 2.0 %collective-permute-done.8.there_ref = f32[256,256]{1,0:T(8,128)S(1)} collective-permute-done((f32[256,256]{1,0:T(8,128)S(1)}, f32[256,256]{1,0:T(8,128)S(1)}, u32[]{:S(2)}, u32[]{:S(2)}) %collective-permute-start.8) | collective-permute-done | bytes 262176 | tf_op jit(solution)/shard_map/ppermute | solution.py:37
  36.6 0.4 apply.18.here_ref
  37.0 2.2 %collective-permute-start.9 = (f32[256,256]{1,0:T(8,128)S(1)}, f32[256,256]{1,0:T(8,128)S(1)}, u32[]{:S(2)}, u32[]{:S(2)}) collective-permute-start(f32[256,256]{1,0:T(8,128)S(1)} %apply.18.here_ref), channel_id=1, source_target_pairs={{0,8},{1,9},{2,10},{3,11},{4,12},{5,13},{6,14},{7,15},{8,0},{9,1},... | collective-permute-start | bytes 786440 | tf_op jit(solution)/shard_map/ppermute | solution.py:37
  39.2 0.0 collective-permute-done.5.there_ref
  39.2 0.6 apply.16.here_ref
  39.8 3.7 %collective-permute-start.6 = (f32[256,384]{1,0:T(8,128)S(1)}, f32[256,384]{1,0:T(8,128)S(1)}, u32[]{:S(2)}, u32[]{:S(2)}) collective-permute-start(f32[256,384]{1,0:T(8,128)S(1)} %apply.16.here_ref), channel_id=1, source_target_pairs={{0,128},{16,144},{32,160},{48,176},{64,192},{80,208},{96,224},{112... | collective-permute-start | bytes 1179656 | tf_op jit(solution)/shard_map/ppermute | solution.py:37
  43.5 0.0 collective-permute-done.13.there_ref
  43.5 0.4 apply.22.here_ref
  43.9 3.1 %collective-permute-start.14 = (f32[256,256]{1,0:T(8,128)S(1)}, f32[256,256]{1,0:T(8,128)S(1)}, u32[]{:S(2)}, u32[]{:S(2)}) collective-permute-start(f32[256,256]{1,0:T(8,128)S(1)} %apply.22.here_ref), channel_id=1, source_target_pairs={{0,128},{16,144},{32,160},{48,176},{64,192},{80,208},{96,224},{112... | collective-permute-start | bytes 786440 | tf_op jit(solution)/shard_map/ppermute | solution.py:37
  47.0 0.0 collective-permute-done.9.there_ref
  47.0 0.4 apply.19.here_ref
  47.4 3.4 %collective-permute-start.10 = (f32[256,256]{1,0:T(8,128)S(1)}, f32[256,256]{1,0:T(8,128)S(1)}, u32[]{:S(2)}, u32[]{:S(2)}) collective-permute-start(f32[256,256]{1,0:T(8,128)S(1)} %apply.19.here_ref), channel_id=1, source_target_pairs={{0,128},{16,144},{32,160},{48,176},{64,192},{80,208},{96,224},{112... | collective-permute-start | bytes 786440 | tf_op jit(solution)/shard_map/ppermute | solution.py:37
  50.9 5.2 %collective-permute-start = (f32[256,128]{1,0:T(8,128)S(1)}, f32[256,128]{1,0:T(8,128)S(1)}, u32[]{:S(2)}, u32[]{:S(2)}) collective-permute-start(f32[256,128]{1,0:T(8,128)S(1)} %get-tuple-element.9.here_ref), channel_id=1, source_target_pairs={{0,256},{16,272},{32,288},{48,304},{64,320},{80,336},{96,352},{112... | collective-permute-start | bytes 393224 | tf_op jit(solution)/shard_map/ppermute | solution.py:37
  56.1 0.0 collective-permute-done.6.there_ref
  56.1 0.6 apply.17.here_ref
  56.7 7.7 %collective-permute-start.7 = (f32[256,384]{1,0:T(8,128)S(1)}, f32[256,384]{1,0:T(8,128)S(1)}, u32[]{:S(2)}, u32[]{:S(2)}) collective-permute-start(f32[256,384]{1,0:T(8,128)S(1)} %apply.17.here_ref), channel_id=1, source_target_pairs={{0,4},{1,5},{2,6},{3,7},{4,0},{5,1},{6,2},{7,3},{8,12},{9,13},{10,... | collective-permute-start | bytes 1179656 | tf_op jit(solution)/shard_map/ppermute | solution.py:37
  64.4 2.4 %collective-permute-done.there_ref = f32[256,128]{1,0:T(8,128)S(1)} collective-permute-done((f32[256,128]{1,0:T(8,128)S(1)}, f32[256,128]{1,0:T(8,128)S(1)}, u32[]{:S(2)}, u32[]{:S(2)}) %collective-permute-start) | collective-permute-done | bytes 131104 | tf_op jit(solution)/shard_map/ppermute | solution.py:37
  66.8 0.4 apply.12.here_ref
  67.1 3.4 %collective-permute-start.1 = (f32[256,128]{1,0:T(8,128)S(1)}, f32[256,128]{1,0:T(8,128)S(1)}, u32[]{:S(2)}, u32[]{:S(2)}) collective-permute-start(f32[256,128]{1,0:T(8,128)S(1)} %apply.12.here_ref), channel_id=1, source_target_pairs={{0,8},{1,9},{2,10},{3,11},{4,12},{5,13},{6,14},{7,15},{8,0},{9,1},... | collective-permute-start | bytes 393224 | tf_op jit(solution)/shard_map/ppermute | solution.py:37
  70.5 0.0 collective-permute-done.14.there_ref
  70.5 0.4 apply.23.here_ref
  70.9 7.7 %collective-permute-start.15 = (f32[256,256]{1,0:T(8,128)S(1)}, f32[256,256]{1,0:T(8,128)S(1)}, u32[]{:S(2)}, u32[]{:S(2)}) collective-permute-start(f32[256,256]{1,0:T(8,128)S(1)} %apply.23.here_ref), channel_id=1, source_target_pairs={{0,4},{1,5},{2,6},{3,7},{4,0},{5,1},{6,2},{7,3},{8,12},{9,13},{10,... | collective-permute-start | bytes 786440 | tf_op jit(solution)/shard_map/ppermute | solution.py:37
  78.7 0.0 collective-permute-done.10.there_ref
  78.7 0.4 apply.20.here_ref
  79.1 2.0 %collective-permute-start.11 = (f32[256,256]{1,0:T(8,128)S(1)}, f32[256,256]{1,0:T(8,128)S(1)}, u32[]{:S(2)}, u32[]{:S(2)}) collective-permute-start(f32[256,256]{1,0:T(8,128)S(1)} %apply.20.here_ref), channel_id=1, source_target_pairs={{0,4},{1,5},{2,6},{3,7},{4,0},{5,1},{6,2},{7,3},{8,12},{9,13},{10,... | collective-permute-start | bytes 786440 | tf_op jit(solution)/shard_map/ppermute | solution.py:37
  81.1 0.0 collective-permute-done.1.there_ref
  81.1 0.4 apply.13.here_ref
  81.5 2.1 %collective-permute-start.2 = (f32[256,128]{1,0:T(8,128)S(1)}, f32[256,128]{1,0:T(8,128)S(1)}, u32[]{:S(2)}, u32[]{:S(2)}) collective-permute-start(f32[256,128]{1,0:T(8,128)S(1)} %apply.13.here_ref), channel_id=1, source_target_pairs={{0,128},{16,144},{32,160},{48,176},{64,192},{80,208},{96,224},{112... | collective-permute-start | bytes 393224 | tf_op jit(solution)/shard_map/ppermute | solution.py:37
  83.6 4.7 %collective-permute-done.2.there_ref = f32[256,128]{1,0:T(8,128)S(1)} collective-permute-done((f32[256,128]{1,0:T(8,128)S(1)}, f32[256,128]{1,0:T(8,128)S(1)}, u32[]{:S(2)}, u32[]{:S(2)}) %collective-permute-start.2) | collective-permute-done | bytes 131104 | tf_op jit(solution)/shard_map/ppermute | solution.py:37
  88.3 0.4 apply.14.here_ref
  88.7 7.7 %collective-permute-start.3 = (f32[256,128]{1,0:T(8,128)S(1)}, f32[256,128]{1,0:T(8,128)S(1)}, u32[]{:S(2)}, u32[]{:S(2)}) collective-permute-start(f32[256,128]{1,0:T(8,128)S(1)} %apply.14.here_ref), channel_id=1, source_target_pairs={{0,4},{1,5},{2,6},{3,7},{4,0},{5,1},{6,2},{7,3},{8,12},{9,13},{10,... | collective-permute-start | bytes 393224 | tf_op jit(solution)/shard_map/ppermute | solution.py:37
  96.4 1.9 %collective-permute-done.15.there_ref = f32[256,256]{1,0:T(8,128)S(1)} collective-permute-done((f32[256,256]{1,0:T(8,128)S(1)}, f32[256,256]{1,0:T(8,128)S(1)}, u32[]{:S(2)}, u32[]{:S(2)}) %collective-permute-start.15) | collective-permute-done | bytes 262176 | tf_op jit(solution)/shard_map/ppermute | solution.py:37
  98.4 1.1 finish.4.refs_0_
  99.5 7.8 %collective-permute-done.11.there_ref = f32[256,256]{1,0:T(8,128)S(1)} collective-permute-done((f32[256,256]{1,0:T(8,128)S(1)}, f32[256,256]{1,0:T(8,128)S(1)}, u32[]{:S(2)}, u32[]{:S(2)}) %collective-permute-start.11) | collective-permute-done | bytes 262176 | tf_op jit(solution)/shard_map/ppermute | solution.py:37
  107.3 1.1 finish.5.refs_0_
  108.4 1.3 %finish.6.refs_0_ = f32[1,1,256,1024]{3,2,1,0:T(8,128)} custom-call(f32[4,1,1,256,512]{4,3,2,1,0:T(8,128)S(1)} %copy-done, f32[256,384]{1,0:T(8,128)S(1)} %apply.17.here_ref, f32[256,384]{1,0:T(8,128)S(1)} %collective-permute-done.7.there_ref, f32[1,1,256,1024]{3,2,1,0:T(8,128)} %finish.5.refs_0_), custom_call_target="tpu_custom_call", output_to_operand_aliasing={{}: (3, {})} | custom-call | flops 301989888 | bytes 1179648 | tf_op jit(solution)/shard_map/finish/pallas_call | solution.py:102
  109.8 1.0 finish.7
  (5 shorter events, 0.0 us)
Async XLA Ops:
  0.0 1.2 %copy-start.1 = (f32[1,1,256,1024]{3,2,1,0:T(8,128)S(1)}, f32[1,1,256,1024]{3,2,1,0:T(8,128)}, u32[]{:S(2)}) copy-start(f32[1,1,256,1024]{3,2,1,0:T(8,128)} %param.2) | copy-start | bytes 3145732
  1.2 14.5 %copy-start = (f32[4,1,1,256,512]{4,3,2,1,0:T(8,128)S(1)}, f32[4,1,1,256,512]{4,3,2,1,0:T(8,128)}, u32[]{:S(2)}) copy-start(f32[4,1,1,256,512]{4,3,2,1,0:T(8,128)} %blocks_ref.31) | copy-start | bytes 6291460
  1.4 14.4 %collective-permute-start.4 = (f32[256,384]{1,0:T(8,128)S(1)}, f32[256,384]{1,0:T(8,128)S(1)}, u32[]{:S(2)}, u32[]{:S(2)}) collective-permute-start(f32[256,384]{1,0:T(8,128)S(1)} %get-tuple-element.10.here_ref), channel_id=1, source_target_pairs={{0,256},{16,272},{32,288},{48,304},{64,320},{80,336},{96,352},{112... | collective-permute-start | bytes 1179656 | tf_op jit(solution)/shard_map/ppermute | solution.py:37
  16.3 22.8 %collective-permute-start.5 = (f32[256,384]{1,0:T(8,128)S(1)}, f32[256,384]{1,0:T(8,128)S(1)}, u32[]{:S(2)}, u32[]{:S(2)}) collective-permute-start(f32[256,384]{1,0:T(8,128)S(1)} %apply.15.here_ref), channel_id=1, source_target_pairs={{0,8},{1,9},{2,10},{3,11},{4,12},{5,13},{6,14},{7,15},{8,0},{9,1},... | collective-permute-start | bytes 1179656 | tf_op jit(solution)/shard_map/ppermute | solution.py:37
  20.6 11.6 %collective-permute-start.12 = (f32[256,256]{1,0:T(8,128)S(1)}, f32[256,256]{1,0:T(8,128)S(1)}, u32[]{:S(2)}, u32[]{:S(2)}) collective-permute-start(f32[256,256]{1,0:T(8,128)S(1)} %get-tuple-element.12.here_ref), channel_id=1, source_target_pairs={{0,256},{16,272},{32,288},{48,304},{64,320},{80,336},{96,352},{112... | collective-permute-start | bytes 786440 | tf_op jit(solution)/shard_map/ppermute | solution.py:37
  25.6 11.0 %collective-permute-start.8 = (f32[256,256]{1,0:T(8,128)S(1)}, f32[256,256]{1,0:T(8,128)S(1)}, u32[]{:S(2)}, u32[]{:S(2)}) collective-permute-start(f32[256,256]{1,0:T(8,128)S(1)} %get-tuple-element.11.here_ref), channel_id=1, source_target_pairs={{0,256},{16,272},{32,288},{48,304},{64,320},{80,336},{96,352},{112... | collective-permute-start | bytes 786440 | tf_op jit(solution)/shard_map/ppermute | solution.py:37
  32.6 10.8 %collective-permute-start.13 = (f32[256,256]{1,0:T(8,128)S(1)}, f32[256,256]{1,0:T(8,128)S(1)}, u32[]{:S(2)}, u32[]{:S(2)}) collective-permute-start(f32[256,256]{1,0:T(8,128)S(1)} %apply.21.here_ref), channel_id=1, source_target_pairs={{0,8},{1,9},{2,10},{3,11},{4,12},{5,13},{6,14},{7,15},{8,0},{9,1},... | collective-permute-start | bytes 786440 | tf_op jit(solution)/shard_map/ppermute | solution.py:37
  37.0 10.1 %collective-permute-start.9 = (f32[256,256]{1,0:T(8,128)S(1)}, f32[256,256]{1,0:T(8,128)S(1)}, u32[]{:S(2)}, u32[]{:S(2)}) collective-permute-start(f32[256,256]{1,0:T(8,128)S(1)} %apply.18.here_ref), channel_id=1, source_target_pairs={{0,8},{1,9},{2,10},{3,11},{4,12},{5,13},{6,14},{7,15},{8,0},{9,1},... | collective-permute-start | bytes 786440 | tf_op jit(solution)/shard_map/ppermute | solution.py:37
  39.8 16.3 %collective-permute-start.6 = (f32[256,384]{1,0:T(8,128)S(1)}, f32[256,384]{1,0:T(8,128)S(1)}, u32[]{:S(2)}, u32[]{:S(2)}) collective-permute-start(f32[256,384]{1,0:T(8,128)S(1)} %apply.16.here_ref), channel_id=1, source_target_pairs={{0,128},{16,144},{32,160},{48,176},{64,192},{80,208},{96,224},{112... | collective-permute-start | bytes 1179656 | tf_op jit(solution)/shard_map/ppermute | solution.py:37
  43.9 26.6 %collective-permute-start.14 = (f32[256,256]{1,0:T(8,128)S(1)}, f32[256,256]{1,0:T(8,128)S(1)}, u32[]{:S(2)}, u32[]{:S(2)}) collective-permute-start(f32[256,256]{1,0:T(8,128)S(1)} %apply.22.here_ref), channel_id=1, source_target_pairs={{0,128},{16,144},{32,160},{48,176},{64,192},{80,208},{96,224},{112... | collective-permute-start | bytes 786440 | tf_op jit(solution)/shard_map/ppermute | solution.py:37
  47.4 31.2 %collective-permute-start.10 = (f32[256,256]{1,0:T(8,128)S(1)}, f32[256,256]{1,0:T(8,128)S(1)}, u32[]{:S(2)}, u32[]{:S(2)}) collective-permute-start(f32[256,256]{1,0:T(8,128)S(1)} %apply.19.here_ref), channel_id=1, source_target_pairs={{0,128},{16,144},{32,160},{48,176},{64,192},{80,208},{96,224},{112... | collective-permute-start | bytes 786440 | tf_op jit(solution)/shard_map/ppermute | solution.py:37
  50.9 15.9 %collective-permute-start = (f32[256,128]{1,0:T(8,128)S(1)}, f32[256,128]{1,0:T(8,128)S(1)}, u32[]{:S(2)}, u32[]{:S(2)}) collective-permute-start(f32[256,128]{1,0:T(8,128)S(1)} %get-tuple-element.9.here_ref), channel_id=1, source_target_pairs={{0,256},{16,272},{32,288},{48,304},{64,320},{80,336},{96,352},{112... | collective-permute-start | bytes 393224 | tf_op jit(solution)/shard_map/ppermute | solution.py:37
  56.7 51.8 %collective-permute-start.7 = (f32[256,384]{1,0:T(8,128)S(1)}, f32[256,384]{1,0:T(8,128)S(1)}, u32[]{:S(2)}, u32[]{:S(2)}) collective-permute-start(f32[256,384]{1,0:T(8,128)S(1)} %apply.17.here_ref), channel_id=1, source_target_pairs={{0,4},{1,5},{2,6},{3,7},{4,0},{5,1},{6,2},{7,3},{8,12},{9,13},{10,... | collective-permute-start | bytes 1179656 | tf_op jit(solution)/shard_map/ppermute | solution.py:37
  67.1 14.0 %collective-permute-start.1 = (f32[256,128]{1,0:T(8,128)S(1)}, f32[256,128]{1,0:T(8,128)S(1)}, u32[]{:S(2)}, u32[]{:S(2)}) collective-permute-start(f32[256,128]{1,0:T(8,128)S(1)} %apply.12.here_ref), channel_id=1, source_target_pairs={{0,8},{1,9},{2,10},{3,11},{4,12},{5,13},{6,14},{7,15},{8,0},{9,1},... | collective-permute-start | bytes 393224 | tf_op jit(solution)/shard_map/ppermute | solution.py:37
  70.9 27.5 %collective-permute-start.15 = (f32[256,256]{1,0:T(8,128)S(1)}, f32[256,256]{1,0:T(8,128)S(1)}, u32[]{:S(2)}, u32[]{:S(2)}) collective-permute-start(f32[256,256]{1,0:T(8,128)S(1)} %apply.23.here_ref), channel_id=1, source_target_pairs={{0,4},{1,5},{2,6},{3,7},{4,0},{5,1},{6,2},{7,3},{8,12},{9,13},{10,... | collective-permute-start | bytes 786440 | tf_op jit(solution)/shard_map/ppermute | solution.py:37
  79.1 28.3 %collective-permute-start.11 = (f32[256,256]{1,0:T(8,128)S(1)}, f32[256,256]{1,0:T(8,128)S(1)}, u32[]{:S(2)}, u32[]{:S(2)}) collective-permute-start(f32[256,256]{1,0:T(8,128)S(1)} %apply.20.here_ref), channel_id=1, source_target_pairs={{0,4},{1,5},{2,6},{3,7},{4,0},{5,1},{6,2},{7,3},{8,12},{9,13},{10,... | collective-permute-start | bytes 786440 | tf_op jit(solution)/shard_map/ppermute | solution.py:37
  81.5 6.9 %collective-permute-start.2 = (f32[256,128]{1,0:T(8,128)S(1)}, f32[256,128]{1,0:T(8,128)S(1)}, u32[]{:S(2)}, u32[]{:S(2)}) collective-permute-start(f32[256,128]{1,0:T(8,128)S(1)} %apply.13.here_ref), channel_id=1, source_target_pairs={{0,128},{16,144},{32,160},{48,176},{64,192},{80,208},{96,224},{112... | collective-permute-start | bytes 393224 | tf_op jit(solution)/shard_map/ppermute | solution.py:37
  88.7 21.1 %collective-permute-start.3 = (f32[256,128]{1,0:T(8,128)S(1)}, f32[256,128]{1,0:T(8,128)S(1)}, u32[]{:S(2)}, u32[]{:S(2)}) collective-permute-start(f32[256,128]{1,0:T(8,128)S(1)} %apply.14.here_ref), channel_id=1, source_target_pairs={{0,4},{1,5},{2,6},{3,7},{4,0},{5,1},{6,2},{7,3},{8,12},{9,13},{10,... | collective-permute-start | bytes 393224 | tf_op jit(solution)/shard_map/ppermute | solution.py:37
